TPU v7x, 128 devices: a whole 4x4x4 slice. The times are simulated.
128 devices in a mesh: dp: 32 (over x, y, core), tensor: 4 (over z).
Axes of the slice: x: 4, y: 4, z: 4, core: 2. Of those that a mesh axis runs over, the one named last changes fastest.
Arguments:
- activations: bfloat16 [32, 1536, 2048], P('dp', 'tensor'), may hold values from -6 to 6
- upstream_grad: bfloat16 [32, 1536, 4096], P('dp', None, 'tensor'), may hold values from -0.15625 to 0.15625
- feedback: bfloat16 [32, 2048, 4096], P('dp', None, 'tensor'), may hold values from -3 to 3
- selected: int32 [32, 4, 2], P('dp', 'tensor'), may hold values from -1 to 255, as said below
- cycle_values: bfloat16 [8, 4, 64, 64, 128], P(None, 'tensor'), may hold values from -6 to 6
- cycle_blocks: int32 [8, 4, 64], P(None, 'tensor'), may hold values from -1 to 255, as said below
- cycle_position: int32 [1], replicated, may hold values from 0 to 7
Outputs:
- update_dir: bfloat16 [2048, 4096], P(None, 'tensor')
- new_feedback: bfloat16 [32, 2048, 4096], P('dp', None, 'tensor')
- newest_values: bfloat16 [4, 64, 64, 128], P('tensor')
Inputs may be any that keep to these rules, and one draw needn't show every extreme that they name: `selected`: for each replica and tensor shard, the 2 entries hold 1 to 2 distinct block numbers first, then -1; in every tensor shard some replica lists 2 blocks. `cycle_blocks`: within each slot and tensor shard, entries r * 2 to r * 2 + 1 hold 1 to 2 distinct block numbers first, then -1; in every slot and shard some group of 2 entries is full.
All inputs are finite; a program needn't handle non-finite values.
Results may differ from a plain program's by a relative error of at most 0.0023.
Values may be sent and summed in bfloat16 or wider, within the bound.
No kernel may reach another device: no remote copies, remote signals or barrier semaphores. Data moves between devices by JAX's collectives and lax.ppermute only.
A program may use at most 192 MiB of HBM per device.

v0:
```python
import jax
import jax.numpy as jnp
from jax import lax
from jax.sharding import PartitionSpec as P

D = 2048
BH = 64
BW = 128
SLOTS = 8


decay_first = 0.9
decay_second = 0.999
epsilon = 0.001


def to_blocks(matrix):
    row_blocks = matrix.shape[0] // BH
    col_blocks = matrix.shape[1] // BW
    return (
        matrix.reshape(row_blocks, BH, col_blocks, BW)
        .transpose(0, 2, 1, 3)
        .reshape(row_blocks * col_blocks, BH, BW)
    )


def from_blocks(blocks, height, breadth):
    return (
        blocks.reshape(height // BH, breadth // BW, BH, BW)
        .transpose(0, 2, 1, 3)
        .reshape(height, breadth)
    )


def local(
    activations, upstream_grad, feedback, selected, cycle_values, cycle_blocks, cycle_position
):
    token_rows = activations[0]
    upstream = upstream_grad[0]
    shard_width = upstream.shape[1]
    contract = (((0,), (0,)), ((), ()))
    gathered = lax.all_gather(token_rows, "tensor", axis=0, tiled=True)
    gradient = lax.dot_general(gathered, upstream, contract, preferred_element_type=jnp.float32)
    accumulated = gradient + feedback[0].astype(jnp.float32)
    blocks = to_blocks(accumulated)
    block_total = blocks.shape[0]
    chosen = selected[0, 0]
    is_live = chosen >= 0
    safe_index = jnp.where(is_live, chosen, 0)
    outgoing = (blocks[safe_index] * is_live[:, None, None]).astype(jnp.bfloat16)
    cleared = jnp.any(jnp.arange(block_total)[:, None] == chosen[None, :], axis=1)
    remaining = jnp.where(cleared[:, None, None], 0.0, blocks)
    new_feedback = from_blocks(remaining, D, shard_width).astype(jnp.bfloat16)[None]
    all_values, all_blocks = (
        lax.all_gather(outgoing, "dp", axis=0, tiled=True),
        lax.all_gather(chosen, "dp", axis=0, tiled=True),
    )
    entry_total = all_values.shape[0]
    position = cycle_position[0]
    targets = jnp.arange(block_total)
    first_moment = jnp.zeros((block_total, BH * BW), jnp.float32)
    second_moment = jnp.zeros((block_total, BH * BW), jnp.float32)
    for slot_number in range(SLOTS):
        newest = position == slot_number
        values = jnp.where(newest, all_values, cycle_values[slot_number, 0])
        listed = jnp.where(newest, all_blocks, cycle_blocks[slot_number, 0])
        onehot = (targets[:, None] == listed[None, :]).astype(jnp.bfloat16)
        densified = jnp.dot(
            onehot, values.reshape(entry_total, BH * BW), preferred_element_type=jnp.float32
        )
        slot_age = jnp.mod(position - slot_number, SLOTS).astype(jnp.float32)
        weight_first = (1.0 - decay_first) * jnp.power(decay_first, slot_age)
        weight_second = (1.0 - decay_second) * jnp.power(decay_second, slot_age)
        first_moment = first_moment + weight_first * densified
        second_moment = second_moment + weight_second * (densified * densified)
    update = (
        (first_moment / (jnp.sqrt(second_moment) + epsilon))
        .astype(jnp.bfloat16)
        .reshape(block_total, BH, BW)
    )
    update_dir = from_blocks(update, D, shard_width)
    return (update_dir, new_feedback, all_values[None])


def solution(mesh):
    placed = (
        P("dp", "tensor", None),
        P("dp", None, "tensor"),
        P("dp", None, "tensor"),
        P("dp", "tensor", None),
        P(None, "tensor", None, None, None),
        P(None, "tensor", None),
        P(),
    )
    return jax.shard_map(
        local,
        mesh=mesh,
        in_specs=placed,
        out_specs=(P(None, "tensor"), P("dp", None, "tensor"), P("tensor", None, None, None)),
        check_vma=False,
    )
```

profile of v0, /device:TPU:1, one launch (start us, length us, event | category | flops | bytes accessed | tf_op | source)
XLA Modules:
  0.0 211.0 jit_solution(4553705174519842768)
XLA Ops:
  7.2 0.0 copy-start
  7.2 0.0 all-gather.7.cloned.1.call-start
  7.2 0.7 all-gather.7.cloned.1.call-update
  7.9 0.0 all-gather.5.cloned.1.call-start
  8.0 0.9 compare_reduce_fusion
  8.9 0.1 broadcast_in_dim.20
  9.0 0.7 fusion.44
  9.6 0.7 compare_convert_fusion
  10.3 68.5 %all-gather.7.cloned.1.call-done = bf16[1,1536,2048]{2,1,0:T(8,128)(2,1)} async-done(((bf16[1,384,2048]{2,1,0:T(8,128)(2,1)}), bf16[1,1536,2048]{2,1,0:T(8,128)(2,1)}) %all-gather.7.cloned.1.call-update) | async-done | bytes 6291472 | tf_op jit(solution)/shard_map/all_gather | solution.py:42
  78.8 0.6 broadcast_in_dim.21
  79.4 0.0 copy-done
  79.4 12.2 %fusion.3 = (bf16[1,2048,1024]{2,1,0:T(8,128)(2,1)}, f32[256,8,8,128]{3,1,2,0:T(8,128)S(1)}) fusion(pred[256,8,8,128]{3,2,1,0:T(8,128)(4,1)S(1)} %bitcast.150, bf16[1,2048,1024]{2,1,0:T(8,128)(2,1)} %param.9, bf16[1,1536,1024]{2,1,0:T(8,128)(2,1)S(1)} %copy-done, bf16[1,1536,2048]{2,1,0:T(8,128)(2,1)} %all-gather.7.cloned.1.call-done), kind=kOutput, calls=%fused_computation.7 | convolution fusion | flops 6450839552 | bytes 28311552 | tf_op jit(solution)/shard_map/dot_general | solution.py:43
  91.6 2.1 copy.13
  93.7 0.0 copy-start.5
  93.7 0.0 copy-start.4
  93.8 0.0 copy-start.3
  93.8 4.9 %copy.12 = f32[32,64,8,128]{3,1,2,0:T(8,128)} copy(f32[32,64,8,128]{3,2,1,0:T(8,128)S(1)} %bitcast.138) | data formatting | bytes 16777216 | tf_op jit(solution)/shard_map/reshape | solution.py:21
  98.6 3.9 %gather_fusion = f32[2,64,128]{2,1,0:T(8,128)S(1)} fusion(f32[256,64,128]{2,1,0:T(8,128)} %bitcast.139, s32[1024]{0:T(1024)S(1)} %pad_clamp_fusion), kind=kCustom, calls=%fused_computation | custom fusion | bytes 131080 | tf_op jit(solution)/shard_map/gather | solution.py:50
  102.6 0.7 multiply_convert_fusion
  103.3 0.0 all-gather.5.cloned.1.call-update
  104.7 0.0 copy-done.5
  104.7 0.6 dynamic-slice
  106.0 0.0 copy-done.4
  106.0 0.1 bitcast_dynamic-update-slice_fusion
  106.1 13.3 %all-reduce = s32[64]{0:T(128)S(1)} all-reduce(s32[64]{0:T(128)S(1)} %bitcast_dynamic-update-slice_fusion), channel_id=2, replica_groups=mesh['dp'=32,'tensor'=4] {'dp'}, use_global_device_ids=true, to_apply=%add | all-reduce | flops 64 | bytes 512
  119.4 0.0 copy-done.3
  119.4 27.6 %all-gather.5.cloned.1.call-done = bf16[64,64,128]{2,1,0:T(8,128)(2,1)} async-done(((bf16[2,64,128]{2,1,0:T(8,128)(2,1)}), bf16[64,64,128]{2,1,0:T(8,128)(2,1)}) %all-gather.5.cloned.1.call-update) | async-done | bytes 1048592 | tf_op jit(solution)/shard_map/all_gather | solution.py:55
  147.0 4.0 %bitcast_select_fusion = (bf16[64,64,128]{2,1,0:T(8,128)(2,1)S(1)}, bf16[64,64,128]{2,1,0:T(8,128)(2,1)S(1)}, bf16[64,64,128]{2,1,0:T(8,128)(2,1)S(1)}, bf16[64,...) fusion(bf16[64,64,128]{2,1,0:T(8,128)(2,1)} %all-gather.5.clone, ...), kind=kLoop, calls=%fused_computation.33 | loop fusion | flops 4194304 | bytes 17825800 | tf_op jit(solution)/shard_map/jit(_where)/select_n | solution.py:65
  151.1 1.3 fusion.7
  152.3 1.3 fusion.10
  153.6 4.5 %fusion.13 = f32[256,8192]{1,0:T(8,128)} fusion(bf16[8,8,64,128]{3,2,1,0:T(8,128)(2,1)S(1)} %bitcast.144, s32[64]{0:T(128)S(1)} %get-tuple-element.18), kind=kOutput, calls=%fused_computation.18 | convolution fusion | flops 268451840 | bytes 9437440 | tf_op jit(solution)/shard_map/dot_general | solution.py:68
  158.2 4.5 %fusion.16 = f32[256,8192]{1,0:T(8,128)} fusion(bf16[8,8,64,128]{3,2,1,0:T(8,128)(2,1)S(1)} %bitcast.143, s32[64]{0:T(128)S(1)} %get-tuple-element.17), kind=kOutput, calls=%fused_computation.21 | convolution fusion | flops 268451840 | bytes 9437440 | tf_op jit(solution)/shard_map/dot_general | solution.py:68
  162.7 4.5 %fusion.19 = f32[256,8192]{1,0:T(8,128)} fusion(bf16[8,8,64,128]{3,2,1,0:T(8,128)(2,1)S(1)} %bitcast.142, s32[64]{0:T(128)S(1)} %get-tuple-element.16), kind=kOutput, calls=%fused_computation.24 | convolution fusion | flops 268451840 | bytes 9437440 | tf_op jit(solution)/shard_map/dot_general | solution.py:68
  167.2 4.5 %fusion.22 = f32[256,8192]{1,0:T(8,128)} fusion(bf16[8,8,64,128]{3,2,1,0:T(8,128)(2,1)S(1)} %bitcast.141, s32[64]{0:T(128)S(1)} %get-tuple-element.15), kind=kOutput, calls=%fused_computation.27 | convolution fusion | flops 268451840 | bytes 9437440 | tf_op jit(solution)/shard_map/dot_general | solution.py:68
  171.7 4.5 %fusion.25 = f32[256,8192]{1,0:T(8,128)} fusion(bf16[8,8,64,128]{3,2,1,0:T(8,128)(2,1)S(1)} %bitcast.140, s32[64]{0:T(128)S(1)} %get-tuple-element.14), kind=kOutput, calls=%fused_computation.30 | convolution fusion | flops 268451840 | bytes 9437440 | tf_op jit(solution)/shard_map/dot_general | solution.py:68
  176.2 0.0 copy-start.1
  176.2 21.6 %divide_convert_fusion = bf16[256,8192]{1,0:T(8,128)(2,1)} fusion(f32[256,8192]{1,0:T(8,128)S(1)} %fusion.7, f32[256,8192]{1,0:T(8,128)S(1)} %fusion.10, f32[256,8192]{1,0:T(8,128)} %fusion.13, f32[256,8192]{1,0:T(8,128)} %fusion.16, f32[256,8192]{1,0:T(8,128)} %fusion.19, f32[256,8192]{1,0:T(8,128)} %fusion.22, f32[256,8192]{1,0:T(8,128)} %fusion.25, ...), kind=kOutput, calls=%fused_computation.3 | convolution fusion | flops 354435072 | bytes 63963456 | tf_op jit(solution)/shard_map/dot_general | solution.py:68
  197.8 0.0 copy-start.2
  197.8 5.4 %copy.60 = bf16[256,8,8,128]{3,1,2,0:T(8,128)(2,1)} copy(bf16[256,8,8,128]{3,2,1,0:T(8,128)(2,1)} %bitcast.148) | data formatting | bytes 8388608
  203.2 0.0 copy-done.2
  203.2 1.0 copy.64
  204.2 0.0 copy-done.1
  (3 shorter events, 0.0 us)
Async XLA Ops:
  7.2 72.3 %copy-start = (bf16[1,1536,1024]{2,1,0:T(8,128)(2,1)S(1)}, bf16[1,1536,1024]{2,1,0:T(8,128)(2,1)}, u32[]{:S(2)}) copy-start(bf16[1,1536,1024]{2,1,0:T(8,128)(2,1)} %param.8) | copy-start | bytes 9437188
  7.2 71.6 %all-gather.7.cloned.1.call-start = ((), (), s32[]{:S(2)}) async-start(), calls=%async_computation.1 | async-start | bytes 7864320 | tf_op jit(solution)/shard_map/all_gather | solution.py:42
  7.9 139.1 %all-gather.5.cloned.1.call-start = ((), (), s32[]{:S(2)}) async-start(), calls=%async_computation | async-start | bytes 1081344 | tf_op jit(solution)/shard_map/all_gather | solution.py:55
  93.7 11.0 %copy-start.5 = (u32[128]{0:T(128)S(1)}, u32[128]{0:T(128)}, u32[]{:S(2)}) copy-start(u32[128]{0:T(128)} %constant.93) | copy-start | bytes 1540
  93.7 12.3 %copy-start.4 = (s32[1,1,2]{2,1,0:T(1,128)S(1)}, s32[1,1,2]{2,1,0:T(1,128)}, u32[]{:S(2)}) copy-start(s32[1,1,2]{2,1,0:T(1,128)} %param.10) | copy-start | bytes 28
  93.8 25.7 %copy-start.3 = (s32[8,1,64]{2,1,0:T(1,128)S(1)}, s32[8,1,64]{2,1,0:T(1,128)}, u32[]{:S(2)}) copy-start(s32[8,1,64]{2,1,0:T(1,128)} %param.12) | copy-start | bytes 6148
  176.2 28.0 %copy-start.1 = (bf16[1,1536,1024]{2,1,0:T(8,128)(2,1)S(1)}, bf16[1,1536,1024]{2,1,0:T(8,128)(2,1)}, u32[]{:S(2)}) copy-start(bf16[1,1536,1024]{2,1,0:T(8,128)(2,1)} %param.8) | copy-start | bytes 9437188
  197.8 5.4 %copy-start.2 = (bf16[64,64,128]{2,1,0:T(8,128)(2,1)S(1)}, bf16[64,64,128]{2,1,0:T(8,128)(2,1)}, u32[]{:S(2)}) copy-start(bf16[64,64,128]{2,1,0:T(8,128)(2,1)} %all-gather.5.cloned.1.call-done) | copy-start | bytes 3145732
Sparse Core Ops, SparseCore 0:
  9.7 69.0 all-gather.6
  103.4 43.6 all-gather.4
where the time goes:
time: 211 us
  waiting for transfers between devices  96.8 us (46%)
  matrix products  58.9 us (28%)
  local copies, waits for them, and re-layouts  18.6 us (9%)
  between operations  16.3 us (8%)
  blocking collectives  13.3 us (6%)
  other arithmetic  6.92 us (3%)
    all_gather x1, waiting for transfers between devices, local(): gathered = lax.all_gather(token_rows, 'tensor', axis=0, tiled=True)  68.5 us
    dot_general x8, matrix products, local(): jnp.dot(onehot, values.reshape(entry_total, BH * BW), preferred_element_t...  46.7 us
    all_gather x1, waiting for transfers between devices, local(): lax.all_gather(outgoing, 'dp', axis=0, tiled=True)  27.6 us
    unnamed x1, blocking collectives  13.3 us
    dot_general x1, matrix products, local(): lax.dot_general(gathered, upstream, contract, preferred_element_type=jnp....  12.2 us
    unnamed x18, local copies, waits for them, and re-layouts  9.16 us
    reshape x1, local copies, waits for them, and re-layouts, to_blocks(): matrix.reshape(row_blocks, BH, col_blocks, BW).transpose(0, 2, 1, 3)  4.86 us
  transfers between devices with their start and end apart: 2, of which 2 were waited for; matrix products, arithmetic and copies ran while one was open for 1% of the time, Pallas kernels for 0%

commit v1 on v0

v1 whole, which is shorter than its diff:
```python
import functools

import jax
import jax.numpy as jnp
from jax import lax
from jax.experimental import pallas as pl
from jax.experimental.pallas import tpu as pltpu
from jax.sharding import PartitionSpec as P

D = 2048
QS = 1024
BH = 64
BW = 128
K = 2
SLOTS = 8
NBLK = 256
ENTRIES = 64
NX = 4
NY = 4
NC = 2
NZ = 4
N_DP = 32
TOK = 384
ROWS = 1536
NOTE = 16
QUARTER = D // 4
HALF = D // 2
TOTAL = SLOTS * ENTRIES

decay_first = 0.9
decay_second = 0.999
epsilon = 0.001

CONTRACT = (((0,), (0,)), ((), ()))
SMEM = pltpu.SMEM
VMEM = pltpu.VMEM
F32 = jnp.float32
BF16 = jnp.bfloat16


def whole(space):
    return pl.BlockSpec(memory_space=space)


def params(mb):
    return pltpu.CompilerParams(vmem_limit_bytes=mb << 20)


def cost(flops, moved):
    return pl.CostEstimate(flops=1, bytes_accessed=1, transcendentals=0)


def shift(x, axis, size, step):
    return lax.ppermute(x, axis, [(i, (i + step) % size) for i in range(size)])


FLIPS = (0, 1, 3, 2)


def pass_on(x, flip):
    return lax.ppermute(x, "tensor", [(i, i ^ flip) for i in range(NZ)])


def swap(x, flip):
    return jnp.concatenate([x, pass_on(x, flip)])


def dp_index(x, y, c):
    return (x * NY + y) * NC + c


def dp_exchange(value, partner):
    pairs = []
    for x in range(NX):
        for y in range(NY):
            for c in range(NC):
                pairs.append((dp_index(x, y, c), dp_index(*partner(x, y, c))))
    return jnp.concatenate([value, lax.ppermute(value, "dp", pairs)])


def up_rows(up, offset=0, flip=0):
    me = lax.axis_index("tensor").astype(jnp.int32)
    owner = lax.bitwise_xor(lax.rem(me + offset, NZ), flip)
    return up.at[pl.ds(pl.multiple_of(owner * TOK, TOK), TOK), :]


def reply_kernel(asked, tokens, *outs):
    low = lax.broadcasted_iota(jnp.int32, (TOK, BW), 1) < BH
    for i, out in enumerate(outs):
        halves = []
        for k in range(K):
            row = lax.shift_right_logical(jnp.maximum(asked[i * K + k], 0), 3)
            start = pl.multiple_of(lax.shift_right_logical(row, 1) * BW, BW)
            pair = tokens[:, pl.ds(start, BW)].astype(F32)
            turned = pltpu.roll(pair, BH, 1)
            halves.append(jnp.where(lax.bitwise_and(row, 1) == k, pair, turned))
        out[...] = jnp.where(low, halves[0], halves[1]).astype(BF16)


def reply(asked, tokens):
    return pl.pallas_call(
        reply_kernel,
        out_shape=[jax.ShapeDtypeStruct((TOK, K * BH), BF16)] * NZ,
        in_specs=[whole(SMEM), whole(VMEM)],
        out_specs=[whole(VMEM)] * NZ,
        compiler_params=params(4),
        cost_estimate=cost(0, 1 << 20),
        name="reply",
    )(asked, tokens)


def pick_kernel(chosen, up, fb, own, c1, c2, c3, out, block, sem):
    def fetch(k):
        number = jnp.maximum(chosen[k], 0)
        row = pl.multiple_of(lax.shift_right_logical(number, 3) * BH, BH)
        col = pl.multiple_of(lax.bitwise_and(number, 7) * BW, BW)
        return pltpu.make_async_copy(
            fb.at[pl.ds(row, BH), pl.ds(col, BW)], block.at[k], sem.at[k]
        )

    for k in range(K):
        fetch(k).start()
    lane = lax.broadcasted_iota(jnp.int32, (NOTE, BW), 1)
    out[K * BH :, :] = jnp.where(lane == 0, chosen[0], chosen[1]).astype(F32).astype(BF16)
    for k in range(K):
        col = pl.multiple_of(lax.bitwise_and(jnp.maximum(chosen[k], 0), 7) * BW, BW)
        total = jnp.zeros((K * BH, BW), F32)
        for flip, ref in zip(FLIPS, (own, c1, c2, c3)):
            total += lax.dot_general(
                ref[...],
                up_rows(up, flip=flip)[:, pl.ds(col, BW)],
                CONTRACT,
                preferred_element_type=F32,
            )
        fetch(k).wait()
        live = jnp.where(chosen[k] >= 0, 1.0, 0.0)
        value = total[k * BH : (k + 1) * BH] + block[k].astype(F32)
        out[k * BH : (k + 1) * BH, :] = (value * live).astype(BF16)


def pick(chosen, up, fb, parts):
    return pl.pallas_call(
        pick_kernel,
        out_shape=jax.ShapeDtypeStruct((K * BH + NOTE, BW), BF16),
        in_specs=[whole(SMEM), whole(VMEM), whole(pl.ANY)] + [whole(VMEM)] * NZ,
        out_specs=whole(VMEM),
        scratch_shapes=[VMEM((K, BH, BW), BF16), pltpu.SemaphoreType.DMA((K,))],
        compiler_params=params(4),
        cost_estimate=cost(2 * K * 128 * ROWS * BW, 2 << 20),
        name="pick",
    )(chosen, up, fb, *parts)


def old_moments(start, nxt, w1, w2, vals):
    def entry(i):
        slot = lax.shift_right_logical(i, 6)
        following = nxt[i]
        last = lax.shift_right_logical(following, 6) != slot
        value = vals[jnp.minimum(i, TOTAL - 1)].astype(F32)
        return slot, following, value, w1[slot], jnp.where(last, w2[slot], 0.0)

    def more(carry):
        return carry[0] < TOTAL

    def body(carry):
        i, before, m1, m2, acc = carry
        slot, following, value, one, two = entry(i)
        acc = value + jnp.where(slot == before, 1.0, 0.0) * acc
        return following, slot, m1 + one * value, m2 + two * acc * acc, acc

    slot, following, value, one, two = entry(start)
    carry = (following, slot, one * value, two * value * value, value)
    _, _, m1, m2, _ = lax.while_loop(more, body, carry)
    return m1, m2


def direction(m1, m2):
    return (m1 / (jnp.sqrt(m2) + epsilon)).astype(BF16)


WSTEP = 4
WPARTS = 2


def window_kernel(base, head, nxt, w1, w2, vals, *refs):
    out = refs[-1]
    first = (base + pl.program_id(0)) * WSTEP

    def row(q, _):
        place = pl.ds(pl.multiple_of(q * BH, BH), BH)
        for col in range(QS // BW):
            m1, m2 = old_moments(head[(first + q) * 8 + col], nxt, w1, w2, vals)
            out[place, col * BW : (col + 1) * BW] = direction(m1, m2)
        return 0

    lax.fori_loop(0, WSTEP, row, 0)


def window(part, head, nxt, w1, w2, vals, earlier):
    steps = D // BH // WSTEP // WPARTS
    base = part * steps
    extra = [] if earlier is None else [earlier]
    return pl.pallas_call(
        functools.partial(window_kernel, base),
        out_shape=jax.ShapeDtypeStruct((D, QS), BF16),
        grid=(steps,),
        in_specs=[whole(SMEM)] * 4 + [whole(VMEM)] + [whole(pl.ANY)] * len(extra),
        out_specs=pl.BlockSpec((WSTEP * BH, QS), lambda i: (base + i, 0)),
        input_output_aliases={5: 0} if extra else {},
        compiler_params=params(4),
        cost_estimate=cost(1e9, 10 << 20),
        name="window",
    )(head, nxt, w1, w2, vals, *extra)


def newest_kernel(
    head, old_nxt, w1, w2, got, vals, update, out, values,
    staged, listed, ids, nxt, first, seen, in_sem, out_sem,
):
    dp = lax.axis_index("dp").astype(jnp.int32)

    def order(r, _):
        place = place_of(lax.bitwise_xor(r, dp))
        for k in range(K):
            values[r * K + k] = got[place, k * BH : (k + 1) * BH]
        note = got[place, K * BH : K * BH + NOTE, :].astype(F32)
        listed[pl.ds(r, 1), :] = note[:1].astype(jnp.int32)
        return 0

    lax.fori_loop(0, N_DP, order, 0)
    fetch = pltpu.make_async_copy(listed, ids, in_sem)
    fetch.start()

    def clear(b, _):
        seen[b] = -1
        return 0

    lax.fori_loop(0, NBLK, clear, 0, unroll=8)
    fetch.wait()

    def number(e):
        return ids[lax.shift_right_logical(e, 1), lax.bitwise_and(e, 1)]

    def chain(e, _):
        block = number(e)
        nxt[e] = ENTRIES
        first[e] = 0

        @pl.when(block >= 0)
        def _():
            before = seen[block]
            seen[block] = e
            first[e] = jnp.where(before < 0, 1, 0)

            @pl.when(before >= 0)
            def _():
                nxt[before] = e

        return 0

    lax.fori_loop(0, ENTRIES, chain, 0)

    def out_copy(e):
        block = number(e)
        row = pl.multiple_of(lax.shift_right_logical(block, 3) * BH, BH)
        col = pl.multiple_of(lax.bitwise_and(block, 7) * BW, BW)
        return pltpu.make_async_copy(
            staged.at[e], out.at[pl.ds(row, BH), pl.ds(col, BW)], out_sem.at[e]
        )

    def finish(e, _):
        @pl.when(first[e] == 1)
        def _():
            def more(carry):
                return carry[0] < ENTRIES

            def body(carry):
                i, acc = carry
                return nxt[i], acc + values[i].astype(F32)

            m1, m2 = old_moments(head[number(e)], old_nxt, w1, w2, vals)
            _, acc = lax.while_loop(more, body, (nxt[e], values[e].astype(F32)))
            m1 = m1 + (1.0 - decay_first) * acc
            m2 = m2 + (1.0 - decay_second) * (acc * acc)
            staged[e] = direction(m1, m2)
            out_copy(e).start()

        return 0

    lax.fori_loop(0, ENTRIES, finish, 0)

    def drain(e, _):
        @pl.when(first[e] == 1)
        def _():
            out_copy(e).wait()

        return 0

    lax.fori_loop(0, ENTRIES, drain, 0)


def place_of(apart):
    core, y, x = apart & 1, (apart >> 1) & 3, (apart >> 3) & 3
    return core * 16 + (x ^ (x >> 1)) * 4 + (y ^ (y >> 1))


def newest(head, old_nxt, w1, w2, got, vals, update):
    return pl.pallas_call(
        newest_kernel,
        out_shape=(
            jax.ShapeDtypeStruct((D, QS), BF16),
            jax.ShapeDtypeStruct((ENTRIES, BH, BW), BF16),
        ),
        in_specs=[whole(SMEM)] * 4 + [whole(VMEM)] * 2 + [whole(pl.ANY)],
        out_specs=(whole(pl.ANY), whole(VMEM)),
        scratch_shapes=[
            VMEM((ENTRIES, BH, BW), BF16),
            VMEM((N_DP, BW), jnp.int32),
            SMEM((N_DP, BW), jnp.int32),
            SMEM((ENTRIES,), jnp.int32),
            SMEM((ENTRIES,), jnp.int32),
            SMEM((NBLK,), jnp.int32),
            pltpu.SemaphoreType.DMA,
            pltpu.SemaphoreType.DMA((ENTRIES,)),
        ],
        input_output_aliases={6: 0},
        compiler_params=params(4),
        cost_estimate=cost(1e9, 8 << 20),
        name="newest",
    )(head, old_nxt, w1, w2, got, vals, update)


ACC = jax.ShapeDtypeStruct((QUARTER, QS), F32)


def product(tokens, up):
    return lax.dot_general(tokens, up, CONTRACT, preferred_element_type=F32)


def near_total(up, fb, a, pieces, q):
    part = slice(q * QUARTER, (q + 1) * QUARTER)
    total = fb[part, :].astype(F32) + product(a[:, part], up_rows(up)[...])
    for offset, (ref, at) in zip((3, 1), pieces):
        tokens = ref[:, at * QUARTER : (at + 1) * QUARTER]
        total += product(tokens, up_rows(up, offset)[...])
    return total


def middle_kernel(jobs, n_pieces, up, fb, a, *refs):
    pieces, outs = refs[:n_pieces], refs[n_pieces:]
    for (q, right, left), out in zip(jobs, outs):
        near = [(pieces[i], at) for i, at in (right, left)]
        out[...] = near_total(up, fb, a, near, q)


def middle(up, fb, a, pieces, jobs):
    return pl.pallas_call(
        functools.partial(middle_kernel, jobs, len(pieces)),
        out_shape=[ACC] * len(jobs),
        in_specs=[whole(VMEM)] * (3 + len(pieces)),
        out_specs=[whole(VMEM)] * len(jobs),
        compiler_params=params(8),
        cost_estimate=cost(6 * TOK * QUARTER * QS * len(jobs), 4 << 20),
        name="middle",
    )(up, fb, a, *pieces)


NSPLIT = 4


def end_kernel(quarters, chosen, up, *refs):
    n = len(quarters)
    pieces, accs = refs[:n], refs[n : 2 * n]
    out, staged, sem = refs[-3:]
    wide = QS // NSPLIT
    copies = []
    for j, (q, piece, acc) in enumerate(zip(quarters, pieces, accs)):
        for s in range(NSPLIT):
            cols = slice(s * wide, (s + 1) * wide)
            total = acc[:, cols] + product(piece[...], up_rows(up, 2)[:, cols])
            for r in range(QUARTER // BH):
                for c in range(wide // BW):
                    block = (q * QUARTER // BH + r) * 8 + s * (wide // BW) + c
                    cleared = (block == chosen[0]) | (block == chosen[1])
                    part = total[r * BH : (r + 1) * BH, c * BW : (c + 1) * BW]
                    staged[
                        j, r * BH : (r + 1) * BH, s * wide + c * BW : s * wide + (c + 1) * BW
                    ] = jnp.where(cleared, 0.0, part).astype(BF16)
            copies.append(
                pltpu.make_async_copy(
                    staged.at[j, :, cols],
                    out.at[q * QUARTER : (q + 1) * QUARTER, cols],
                    sem.at[j, s],
                )
            )
            copies[-1].start()
    for copy in copies:
        copy.wait()


def end(chosen, up, pieces, accs, quarters, earlier):
    n = len(quarters)
    extra = [] if earlier is None else [earlier]
    return pl.pallas_call(
        functools.partial(end_kernel, quarters),
        out_shape=jax.ShapeDtypeStruct((D, QS), BF16),
        in_specs=[whole(SMEM)] + [whole(VMEM)] * (1 + 2 * n) + [whole(pl.ANY)] * len(extra),
        out_specs=whole(pl.ANY),
        scratch_shapes=[VMEM((n, QUARTER, QS), BF16), pltpu.SemaphoreType.DMA((n, NSPLIT))],
        input_output_aliases={2 + 2 * n: 0} if extra else {},
        compiler_params=params(6),
        cost_estimate=cost(2 * n * TOK * QUARTER * QS, 4 << 20),
        name="end",
    )(chosen, up, *pieces, *accs, *extra)


def after(value, *events):
    return lax.optimization_barrier((value, events))[0]


def local(
    activations, upstream_grad, feedback, selected, cycle_values, cycle_blocks, cycle_position
):
    a = activations[0]
    up = upstream_grad[0]
    fb = feedback[0]
    chosen = selected[0, 0]
    position = cycle_position[0]

    slots = jnp.arange(SLOTS)
    listed = jnp.where(slots[:, None] == position, -1, cycle_blocks.reshape(SLOTS, ENTRIES))
    listed = listed.reshape(-1)
    count = jnp.arange(TOTAL)
    place = jnp.arange(TOTAL + 128)
    row = jnp.concatenate([listed, jnp.full((128,), -2, jnp.int32)])
    later = (row[:, None] == listed[None, :]) & (count[None, :] > place[:, None])
    nxt = jnp.min(jnp.where(later, count[None, :], TOTAL), axis=1)
    here = jnp.arange(NBLK)[:, None] == listed[None, :]
    head = jnp.min(jnp.where(here, count[None, :], TOTAL), axis=1)
    table = jnp.arange(2 * SLOTS)
    age = jnp.mod(position - table, SLOTS).astype(F32)
    inside = table < SLOTS
    w1 = jnp.where(inside, (1.0 - decay_first) * jnp.power(decay_first, age), 0.0)
    w2 = jnp.where(inside, (1.0 - decay_second) * jnp.power(decay_second, age), 0.0)
    vals = cycle_values.reshape(TOTAL, BH, BW)

    first_r, first_l = a[:, :QUARTER], a[:, -QUARTER:]
    right_0 = shift(first_r, "tensor", NZ, 1)
    left_0 = shift(first_l, "tensor", NZ, -1)
    known = swap(chosen, 1)
    asked = swap(known, 3)

    parts = reply(asked, a)
    replies = [pass_on(parts[i], flip) for i, flip in enumerate(FLIPS) if flip]
    rest = after(a, parts[1], right_0, left_0)
    right_1 = shift(rest[:, QUARTER:HALF], "tensor", NZ, 1)
    left_1 = shift(rest[:, HALF:-QUARTER], "tensor", NZ, -1)

    outgoing = pick(after(chosen, right_0, left_0), up, fb, [parts[0], *replies])
    rest = after(a, outgoing)
    right_2 = shift(rest[:, HALF:], "tensor", NZ, 1)
    left_2 = shift(rest[:, :HALF], "tensor", NZ, -1)

    got_1 = dp_exchange(outgoing[None], lambda x, y, c: (x, y ^ 1, c))
    update = window(0, after(head, got_1), nxt, w1, w2, vals, None)
    got_1 = after(got_1, update, right_1, left_1)
    got_2 = dp_exchange(got_1, lambda x, y, c: (x, y ^ 3, c))
    got_3 = dp_exchange(got_2, lambda x, y, c: (x ^ 1, y, c))
    update = window(1, after(head, got_2), nxt, w1, w2, vals, update)
    got_4 = dp_exchange(after(got_3, update), lambda x, y, c: (x ^ 3, y, c))
    got = dp_exchange(after(got_4, right_2, left_2), lambda x, y, c: (x, y, c ^ 1))

    far_0 = shift(after(right_0, got_2), "tensor", NZ, 1)
    far_3 = shift(after(left_0, got_2), "tensor", NZ, -1)
    far_1 = shift(right_1[:, :QUARTER], "tensor", NZ, 1)
    far_2 = shift(left_1[:, -QUARTER:], "tensor", NZ, -1)

    update_dir, newest_values = newest(head, nxt, w1, w2, got, vals, update)

    near = [right_0, right_1, right_2, left_0, left_1, left_2]
    q1, q2 = middle(up, fb, a, near, ((1, (1, 0), (5, 1)), (2, (2, 0), (4, 0))))
    q0, q3 = middle(
        up, fb, after(a, far_0, far_3), near, ((0, (0, 0), (5, 0)), (3, (2, 1), (3, 0)))
    )
    merged = end(chosen, up, [far_0, far_3], [q0, q3], (0, 3), None)
    merged = end(chosen, up, [far_1, far_2], [q1, q2], (1, 2), merged)
    return (update_dir, merged[None], newest_values[None])


def solution(mesh):
    placed = (
        P("dp", "tensor", None),
        P("dp", None, "tensor"),
        P("dp", None, "tensor"),
        P("dp", "tensor", None),
        P(None, "tensor", None, None, None),
        P(None, "tensor", None),
        P(),
    )
    return jax.shard_map(
        local,
        mesh=mesh,
        in_specs=placed,
        out_specs=(P(None, "tensor"), P("dp", None, "tensor"), P("tensor", None, None, None)),
        check_vma=False,
    )
```

time: 211 us -> 106 us (0.50)
  waiting for transfers between devices: 96.8 us -> 20.3 us
  matrix products: 58.9 us -> 0 us
  Pallas kernels: 0 us -> 37.3 us
  starting transfers between devices: 0.08 us -> 36 us
  between operations: 16.3 us -> 1.66 us
  blocking collectives: 13.3 us -> 0 us
  local copies, waits for them, and re-layouts: 18.6 us -> 6.79 us
  other arithmetic: 6.92 us -> 3.53 us
    all_gather x2 -> x0, waiting for transfers between devices: 96.1 us -> none  [the longest x1 68.5 us: local(): gathered = lax.all_gather(token_rows, 'tensor', axis=0, tiled=True)]
    dot_general x9 -> x0, matrix products: 58.9 us -> none  [the longest x8 46.7 us: local(): jnp.dot(onehot, values.reshape(entry_total, BH * BW), preferred_element_t...]
    pallas_call x0 -> x9, Pallas kernels: none -> 37.3 us  [the longest x2 11.6 us: window(): pl.pallas_call(functools.partial(window_kernel, base), out_shape=jax.Shap...]
    ppermute x0 -> x20, starting transfers between devices: none -> 36 us  [the longest x5 17.1 us: dp_exchange(): return jnp.concatenate([value, lax.ppermute(value, 'dp', pairs)])]
    ppermute x0 -> x20, waiting for transfers between devices: none -> 20.3 us  [the longest x5 8.06 us: dp_exchange(): return jnp.concatenate([value, lax.ppermute(value, 'dp', pairs)])]
    unnamed x1 -> x0, blocking collectives: 13.3 us -> none
    unnamed x18 -> x16, local copies, waits for them, and re-layouts: 9.16 us -> 4.15 us
    reshape x1, local copies, waits for them, and re-layouts: 4.86 us -> 0.08 us  [local(): cycle_blocks.reshape(SLOTS, ENTRIES)]
  transfers between devices with their start and end apart: 2 -> 20, of which waited for: 2 -> 7; matrix products, arithmetic and copies ran while one was open for 1% -> 6% of each run, Pallas kernels for 0% -> 23%
where the time goes in v1:
time: 106 us
  Pallas kernels  37.3 us (35%)
  starting transfers between devices  36 us (34%)
  waiting for transfers between devices  20.3 us (19%)
  local copies, waits for them, and re-layouts  6.79 us (6%)
  other arithmetic  3.53 us (3%)
  between operations  1.66 us (2%)
    ppermute x5, starting transfers between devices, dp_exchange(): return jnp.concatenate([value, lax.ppermute(value, 'dp', pairs)])  17.1 us
    pallas_call x2, Pallas kernels, window(): pl.pallas_call(functools.partial(window_kernel, base), out_shape=jax.Shap...  11.6 us
    ppermute x10, starting transfers between devices, shift(): return lax.ppermute(x, axis, [(i, (i + step) % size) for i in range(size)])  10.3 us
    pallas_call x1, Pallas kernels, newest(): pl.pallas_call(newest_kernel, out_shape=(jax.ShapeDtypeStruct((D, QS), BF...  8.96 us
    pallas_call x2, Pallas kernels, middle(): pl.pallas_call(functools.partial(middle_kernel, jobs, len(pieces)), out_s...  8.86 us
    ppermute x5, starting transfers between devices, pass_on(): return lax.ppermute(x, 'tensor', [(i, i ^ flip) for i in range(NZ)])  8.55 us
    ppermute x5, waiting for transfers between devices, dp_exchange(): return jnp.concatenate([value, lax.ppermute(value, 'dp', pairs)])  8.06 us
    ppermute x5, waiting for transfers between devices, pass_on(): return lax.ppermute(x, 'tensor', [(i, i ^ flip) for i in range(NZ)])  7.68 us
  transfers between devices with their start and end apart: 20, of which 7 were waited for; matrix products, arithmetic and copies ran while one was open for 6% of the time, Pallas kernels for 23%

profile of v1, /device:TPU:1, one launch (start us, length us, event | category | flops | bytes accessed | tf_op | source)
XLA Modules:
  0.0 105.5 jit_solution(8406415104334677622)
XLA Ops:
  0.6 2.5 %collective-permute-start.2 = (s32[2]{0:T(128)}, s32[2]{0:T(128)}, u32[]{:S(2)}, u32[]{:S(2)}) collective-permute-start(s32[2]{0:T(128)} %bitcast.30), channel_id=1, source_target_pairs={{0,1},{1,0},{2,3},{3,2},{4,5},{5,4},{6,7},{7,6},{8,9},{9,8},{10,11... | collective-permute-start | bytes 32 | tf_op jit(solution)/shard_map/ppermute | solution.py:61
  3.2 2.2 %fusion.5 = (bf16[384,512]{1,0:T(8,128)(2,1)}, bf16[384,512]{1,0:T(8,128)(2,1)}) fusion(bf16[384,2048]{1,0:T(8,128)(2,1)} %bitcast.19), kind=kLoop, calls=%fused_computation.24 | loop fusion | bytes 1572864 | tf_op jit(solution)/shard_map/slice | solution.py:447
  5.4 2.2 %collective-permute-start.1 = (bf16[384,512]{1,0:T(8,128)(2,1)}, bf16[384,512]{1,0:T(8,128)(2,1)S(1)}, u32[]{:S(2)}, u32[]{:S(2)}) collective-permute-start(bf16[384,512]{1,0:T(8,128)(2,1)} %get-tuple-element.49), channel_id=1, source_target_pairs={{0,3},{1,0},{2,1},{3,2},{4,7},{5,4},{6,5},{7,6},{8,11},{9,8},{10,9... | collective-permute-start | bytes 1179656 | tf_op jit(solution)/shard_map/ppermute | solution.py:54
  7.6 0.0 collective-permute-start
  8.3 0.1 broadcast_in_dim.58
  8.4 0.1 broadcast_in_dim.59
  8.5 0.5 broadcast.62
  9.0 1.3 %reduce.3 = s32[8,64]{1,0:T(8,128)S(1)} reduce(s32[8,1,64]{2,1,0:T(1,128)} %param.12, s32[]{:T(128)} %broadcast.62), dimensions={1}, to_apply=%param.12.reduce_sub_computation.3 | reduce | bytes 4100 | tf_op args[5]
  10.3 0.1 reshape.32
  10.4 0.3 select_reduce_fusion.nxt.old_nxt
  10.8 0.0 collective-permute-done.2
  10.8 0.7 pad_add_fusion
  11.5 2.7 %collective-permute-start.3 = (s32[4]{0:T(128)S(1)}, s32[4]{0:T(128)S(1)}, u32[]{:S(2)}, u32[]{:S(2)}) collective-permute-start(s32[4]{0:T(128)S(1)} %pad_add_fusion), channel_id=1, source_target_pairs={{0,3},{1,2},{2,1},{3,0},{4,7},{5,6},{6,5},{7,4},{8,11},{9,10},{10,... | collective-permute-start | bytes 56 | tf_op jit(solution)/shard_map/ppermute | solution.py:61
  14.2 4.3 %collective-permute-done.3 = s32[4]{0:T(128)S(1)} collective-permute-done((s32[4]{0:T(128)S(1)}, s32[4]{0:T(128)S(1)}, u32[]{:S(2)}, u32[]{:S(2)}) %collective-permute-start.3) | collective-permute-done | bytes 48 | tf_op jit(solution)/shard_map/ppermute | solution.py:61
  18.5 0.7 pad_add_fusion.1.asked
  19.3 0.1 select_reduce_fusion.1.head
  19.4 0.0 copy-start.2
  19.4 1.4 %copy-done.2 = bf16[1,384,2048]{2,1,0:T(8,128)(2,1)S(1)} copy-done((bf16[1,384,2048]{2,1,0:T(8,128)(2,1)S(1)}, bf16[1,384,2048]{2,1,0:T(8,128)(2,1)}, u32[]{:S(2)}) %copy-start.2) | copy-done | bytes 1572888
  20.8 1.0 reply.1
  21.8 0.3 collective-permute-start.5
  22.1 0.3 collective-permute-start.6
  22.3 2.8 %collective-permute-start.4 = (bf16[384,128]{1,0:T(8,128)(2,1)S(1)}, bf16[384,128]{1,0:T(8,128)(2,1)S(1)}, u32[]{:S(2)}, u32[]{:S(2)}) collective-permute-start(bf16[384,128]{1,0:T(8,128)(2,1)S(1)} %get-tuple-element.26), channel_id=1, source_target_pairs={{0,1},{1,0},{2,3},{3,2},{4,5},{5,4},{6,7},{7,6},{8,9},{9,8},{10,11... | collective-permute-start | bytes 294920 | tf_op jit(solution)/shard_map/ppermute | solution.py:61
  25.1 0.0 collective-permute-done.1.refs_3_
  25.2 0.0 collective-permute-done.refs_0_
  25.2 2.4 %collective-permute-done.5.c2 = bf16[384,128]{1,0:T(8,128)(2,1)S(1)} collective-permute-done((bf16[384,128]{1,0:T(8,128)(2,1)S(1)}, bf16[384,128]{1,0:T(8,128)(2,1)S(1)}, u32[]{:S(2)}, u32[]{:S(2)}) %collective-permute-start.5) | collective-permute-done | bytes 98336 | tf_op jit(solution)/shard_map/ppermute | solution.py:61
  27.6 0.0 collective-permute-done.6.c3
  27.6 0.9 collective-permute-done.4.c1
  28.5 2.2 %copy-done.4 = bf16[1,2048,1024]{2,1,0:T(8,128)(2,1)S(1)} copy-done((bf16[1,2048,1024]{2,1,0:T(8,128)(2,1)S(1)}, bf16[1,2048,1024]{2,1,0:T(8,128)(2,1)}, u32[]{:S(2)}) %copy-start.4) | copy-done | bytes 4194328
  30.7 1.2 %pick.1 = bf16[144,128]{1,0:T(8,128)(2,1)S(1)} custom-call(s32[2]{0:T(128)S(1)} %bitcast.33, bf16[1536,1024]{1,0:T(8,128)(2,1)S(1)} %bitcast.11, bf16[2048,1024]{1,0:T(8,128)(2,1)S(1)} %bitcast.25, bf16[384,128]{1,0:T(8,128)(2,1)S(1)} %get-tuple-element.25.own, bf16[384,128]{1,0:T(8,128)(2,1)S(1)} %collective-permute-done.4.c1, ...), custom_call_target="tpu_custom_call" | custom-call | flops 1 | bytes 1 | tf_op jit(solution)/shard_map/pick/pallas_call | solution.py:142
  31.9 1.4 %collective-permute-start.7 = (bf16[1,144,128]{2,1,0:T(8,128)(2,1)S(1)}, bf16[1,144,128]{2,1,0:T(8,128)(2,1)S(1)}, u32[]{:S(2)}, u32[]{:S(2)}) collective-permute-start(bf16[1,144,128]{2,1,0:T(8,128)(2,1)S(1)} %bitcast.28), channel_id=1, source_target_pairs={{0,8},{4,12},{8,0},{12,4},{16,24},{20,28},{24,16},{28,20},{32,40},... | collective-permute-start | bytes 110600 | tf_op jit(solution)/shard_map/ppermute | solution.py:78
  33.3 0.1 fusion.4
  33.4 1.2 %collective-permute-start.9 = (bf16[384,512]{1,0:T(8,128)(2,1)S(1)}, bf16[384,512]{1,0:T(8,128)(2,1)S(1)}, u32[]{:S(2)}, u32[]{:S(2)}) collective-permute-start(bf16[384,512]{1,0:T(8,128)(2,1)S(1)} %get-tuple-element.47), channel_id=1, source_target_pairs={{0,3},{1,0},{2,1},{3,2},{4,7},{5,4},{6,5},{7,6},{8,11},{9,8},{10,9... | collective-permute-start | bytes 1179656 | tf_op jit(solution)/shard_map/ppermute | solution.py:54
  34.5 0.4 collective-permute-start.8
  34.9 0.1 fusion.3
  35.0 2.4 %collective-permute-start.14 = (bf16[384,1024]{1,0:T(8,128)(2,1)S(1)}, bf16[384,1024]{1,0:T(8,128)(2,1)S(1)}, u32[]{:S(2)}, u32[]{:S(2)}) collective-permute-start(bf16[384,1024]{1,0:T(8,128)(2,1)S(1)} %get-tuple-element.45), channel_id=1, source_target_pairs={{0,3},{1,0},{2,1},{3,2},{4,7},{5,4},{6,5},{7,6},{8,11},{9,8},{10,9... | collective-permute-start | bytes 2359304 | tf_op jit(solution)/shard_map/ppermute | solution.py:54
  37.4 0.0 collective-permute-start.13
  37.4 0.0 collective-permute-done.7
  37.5 5.8 %window.2.refs_0_ = bf16[2048,1024]{1,0:T(8,128)(2,1)} custom-call(s32[256]{0:T(256)S(1)} %select_reduce_fusion.1.head, s32[640]{0:T(1024)S(1)} %select_reduce_fusion.nxt.old_nxt, f32[16]{0:T(128)S(1)} %get-tuple-element.52.w1, f32[16]{0:T(128)S(1)} %get-tuple-element.51.w2, bf16[512,64,128]{2,1,0:T(8,128)(2,1)S(1)} %bitcast.16), custom_call_target="tpu_custom_call" | custom-call | flops 1 | bytes 1 | tf_op jit(solution)/shard_map/window/pallas_call | solution.py:203
  43.3 0.0 collective-permute-done.9.refs_4_
  43.3 0.0 collective-permute-done.8.refs_1_
  43.3 2.0 %collective-permute-start.10 = (bf16[2,144,128]{2,1,0:T(8,128)(2,1)S(1)}, bf16[2,144,128]{2,1,0:T(8,128)(2,1)S(1)}, u32[]{:S(2)}, u32[]{:S(2)}) collective-permute-start(bf16[2,144,128]{2,1,0:T(8,128)(2,1)S(1)} %pad_maximum_fusion.3), channel_id=1, source_target_pairs={{0,24},{4,28},{8,16},{12,20},{16,8},{20,12},{24,0},{28,4},{32,56},... | collective-permute-start | bytes 221192 | tf_op jit(solution)/shard_map/ppermute | solution.py:78
  45.3 2.8 %collective-permute-done.10 = bf16[2,144,128]{2,1,0:T(8,128)(2,1)S(1)} collective-permute-done((bf16[2,144,128]{2,1,0:T(8,128)(2,1)S(1)}, bf16[2,144,128]{2,1,0:T(8,128)(2,1)S(1)}, u32[]{:S(2)}, u32[]{:S(2)}) %collective-permute-start.10) | collective-permute-done | bytes 73760 | tf_op jit(solution)/shard_map/ppermute | solution.py:78
  48.1 1.3 %collective-permute-start.11 = (bf16[4,144,128]{2,1,0:T(8,128)(2,1)S(1)}, bf16[4,144,128]{2,1,0:T(8,128)(2,1)S(1)}, u32[]{:S(2)}, u32[]{:S(2)}) collective-permute-start(bf16[4,144,128]{2,1,0:T(8,128)(2,1)S(1)} %constant_dynamic-update-slice_fusion), channel_id=1, source_target_pairs={{0,32},{4,36},{8,40},{12,44},{16,48},{20,52},{24,56},{28,60},{32,0... | collective-permute-start | bytes 442376 | tf_op jit(solution)/shard_map/ppermute | solution.py:78
  49.4 5.8 %window.3.update = bf16[2048,1024]{1,0:T(8,128)(2,1)} custom-call(s32[256]{0:T(256)S(1)} %select_reduce_fusion.1.head, s32[640]{0:T(1024)S(1)} %select_reduce_fusion.nxt.old_nxt, f32[16]{0:T(128)S(1)} %get-tuple-element.52.w1, f32[16]{0:T(128)S(1)} %get-tuple-element.51.w2, bf16[512,64,128]{2,1,0:T(8,128)(2,1)S(1)} %bitcast.17, ...), custom_call_target="tpu_custom_call", output_to_operand_aliasing={{}: (5, {})} | custom-call | flops 1 | bytes 1 | tf_op jit(solution)/shard_map/window/pallas_call | solution.py:203
  55.2 0.0 collective-permute-done.11
  55.2 1.9 %collective-permute-start.12 = (bf16[8,144,128]{2,1,0:T(8,128)(2,1)S(1)}, bf16[8,144,128]{2,1,0:T(8,128)(2,1)S(1)}, u32[]{:S(2)}, u32[]{:S(2)}) collective-permute-start(bf16[8,144,128]{2,1,0:T(8,128)(2,1)S(1)} %pad_maximum_fusion.2), channel_id=1, source_target_pairs={{0,96},{4,100},{8,104},{12,108},{16,112},{20,116},{24,120},{28,124... | collective-permute-start | bytes 884744 | tf_op jit(solution)/shard_map/ppermute | solution.py:78
  57.1 5.3 %collective-permute-done.12 = bf16[8,144,128]{2,1,0:T(8,128)(2,1)S(1)} collective-permute-done((bf16[8,144,128]{2,1,0:T(8,128)(2,1)S(1)}, bf16[8,144,128]{2,1,0:T(8,128)(2,1)S(1)}, u32[]{:S(2)}, u32[]{:S(2)}) %collective-permute-start.12) | collective-permute-done | bytes 294944 | tf_op jit(solution)/shard_map/ppermute | solution.py:78
  62.4 0.1 pad_maximum_fusion.1
  62.5 0.0 collective-permute-done.14.refs_5_
  62.5 0.0 collective-permute-done.13.refs_2_
  62.5 10.5 %collective-permute-start.15 = (bf16[16,144,128]{2,1,0:T(8,128)(2,1)S(1)}, bf16[16,144,128]{2,1,0:T(8,128)(2,1)S(1)}, u32[]{:S(2)}, u32[]{:S(2)}) collective-permute-start(bf16[16,144,128]{2,1,0:T(8,128)(2,1)S(1)} %pad_maximum_fusion.1), channel_id=1, source_target_pairs={{0,4},{4,0},{8,12},{12,8},{16,20},{20,16},{24,28},{28,24},{32,36},... | collective-permute-start | bytes 1769480 | tf_op jit(solution)/shard_map/ppermute | solution.py:78
  73.0 0.0 collective-permute-start.18
  73.0 2.7 %collective-permute-start.19 = (bf16[384,512]{1,0:T(8,128)(2,1)S(1)}, bf16[384,512]{1,0:T(8,128)(2,1)S(1)}, u32[]{:S(2)}, u32[]{:S(2)}) collective-permute-start(bf16[384,512]{1,0:T(8,128)(2,1)S(1)} %collective-permute-done.1.refs_3_), channel_id=1, source_target_pairs={{0,3},{1,0},{2,1},{3,2},{4,7},{5,4},{6,5},{7,6},{8,11},{9,8},{10,9... | collective-permute-start | bytes 1179656 | tf_op jit(solution)/shard_map/ppermute | solution.py:54
  75.7 0.0 collective-permute-start.17
  75.7 1.4 %collective-permute-start.16 = (bf16[384,512]{1,0:T(8,128)(2,1)S(1)}, bf16[384,512]{1,0:T(8,128)(2,1)S(1)}, u32[]{:S(2)}, u32[]{:S(2)}) collective-permute-start(bf16[384,512]{1,0:T(8,128)(2,1)S(1)} %collective-permute-done.8.refs_1_), channel_id=1, source_target_pairs={{0,1},{1,2},{2,3},{3,0},{4,5},{5,6},{6,7},{7,4},{8,9},{9,10},{10,1... | collective-permute-start | bytes 1179656 | tf_op jit(solution)/shard_map/ppermute | solution.py:54
  77.2 4.4 %middle.2 = (f32[512,1024]{1,0:T(8,128)S(1)}, f32[512,1024]{1,0:T(8,128)S(1)}) custom-call(bf16[1536,1024]{1,0:T(8,128)(2,1)S(1)} %bitcast.12, bf16[2048,1024]{1,0:T(8,128)(2,1)S(1)} %bitcast.26, bf16[384,2048]{1,0:T(8,128)(2,1)S(1)} %bitcast.23, bf16[384,512]{1,0:T(8,128)(2,1)} %collective-permute-done.refs_0_, ...), custom_call_target="tpu_custom_call" | custom-call | flops 1 | bytes 1 | tf_op jit(solution)/shard_map/middle/pallas_call | solution.py:357
  81.6 3.5 %collective-permute-done.18.refs_0_ = bf16[384,512]{1,0:T(8,128)(2,1)S(1)} collective-permute-done((bf16[384,512]{1,0:T(8,128)(2,1)}, bf16[384,512]{1,0:T(8,128)(2,1)S(1)}, u32[]{:S(2)}, u32[]{:S(2)}) %collective-permute-start.18) | collective-permute-done | bytes 393248 | tf_op jit(solution)/shard_map/ppermute | solution.py:54
  85.1 0.0 collective-permute-done.19.refs_1_
  85.1 4.4 %middle.3 = (f32[512,1024]{1,0:T(8,128)S(1)}, f32[512,1024]{1,0:T(8,128)S(1)}) custom-call(bf16[1536,1024]{1,0:T(8,128)(2,1)S(1)} %bitcast.13, bf16[2048,1024]{1,0:T(8,128)(2,1)S(1)} %bitcast.27, bf16[384,2048]{1,0:T(8,128)(2,1)S(1)} %bitcast.24, bf16[384,512]{1,0:T(8,128)(2,1)} %collective-permute-done.refs_0_, ...), custom_call_target="tpu_custom_call" | custom-call | flops 1 | bytes 1 | tf_op jit(solution)/shard_map/middle/pallas_call | solution.py:357
  89.6 2.9 %end.2.refs_4_ = bf16[2048,1024]{1,0:T(8,128)(2,1)} custom-call(s32[2]{0:T(128)S(1)} %bitcast.34, bf16[1536,1024]{1,0:T(8,128)(2,1)S(1)} %bitcast.14, bf16[384,512]{1,0:T(8,128)(2,1)S(1)} %collective-permute-done.18.refs_0_, bf16[384,512]{1,0:T(8,128)(2,1)S(1)} %collective-permute-done.19.refs_1_, f32[512,1024]{1,0:T(8,128)S(1)} %get-tuple-element.42.refs_2_, ...), custom_call_target="tpu_custom_call" | custom-call | flops 1 | bytes 1 | tf_op jit(solution)/shard_map/end/pallas_call | solution.py:404
  92.4 0.1 pad_maximum_fusion.got
  92.6 1.0 collective-permute-done.16.refs_0_
  93.6 2.9 %end.3 = bf16[2048,1024]{1,0:T(8,128)(2,1)} custom-call(s32[2]{0:T(128)S(1)} %bitcast.35, bf16[1536,1024]{1,0:T(8,128)(2,1)S(1)} %bitcast.15, bf16[384,512]{1,0:T(8,128)(2,1)S(1)} %collective-permute-done.16.refs_0_, bf16[384,512]{1,0:T(8,128)(2,1)S(1)} %collective-permute-done.17.refs_1_, ...), custom_call_target="tpu_custom_call", output_to_operand_aliasing={{}: (6, {})} | custom-call | flops 1 | bytes 1 | tf_op jit(solution)/shard_map/end/pallas_call | solution.py:404
  96.4 9.0 %newest.1 = (bf16[2048,1024]{1,0:T(8,128)(2,1)}, bf16[64,64,128]{2,1,0:T(8,128)(2,1)}) custom-call(s32[256]{0:T(256)S(1)} %select_reduce_fusion.1.head, s32[640]{0:T(1024)S(1)} %select_reduce_fusion.nxt.old_nxt, f32[16]{0:T(128)S(1)} %get-tuple-element.52.w1, f32[16]{0:T(128)S(1)} %get-tuple-element.51.w2, ...), custom_call_target="tpu_custom_call", output_to_operand_aliasing={{0}: (6, {})} | custom-call | flops 1 | bytes 1 | tf_op jit(solution)/shard_map/newest/pallas_call | solution.py:308
  (21 shorter events, 0.1 us)
Async XLA Ops:
  0.6 10.1 %copy-start.6 = (s32[1,1,2]{2,1,0:T(1,128)S(1)}, s32[1,1,2]{2,1,0:T(1,128)}, u32[]{:S(2)}) copy-start(s32[1,1,2]{2,1,0:T(1,128)} %param.10) | copy-start | bytes 28
  0.6 10.1 %collective-permute-start.2 = (s32[2]{0:T(128)}, s32[2]{0:T(128)}, u32[]{:S(2)}, u32[]{:S(2)}) collective-permute-start(s32[2]{0:T(128)} %bitcast.30), channel_id=1, source_target_pairs={{0,1},{1,0},{2,3},{3,2},{4,5},{5,4},{6,7},{7,6},{8,9},{9,8},{10,11... | collective-permute-start | bytes 32 | tf_op jit(solution)/shard_map/ppermute | solution.py:61
  3.2 25.3 %copy-start = (bf16[1,1536,1024]{2,1,0:T(8,128)(2,1)S(1)}, bf16[1,1536,1024]{2,1,0:T(8,128)(2,1)}, u32[]{:S(2)}) copy-start(bf16[1,1536,1024]{2,1,0:T(8,128)(2,1)} %param.8) | copy-start | bytes 9437188
  5.4 19.8 %collective-permute-start.1 = (bf16[384,512]{1,0:T(8,128)(2,1)}, bf16[384,512]{1,0:T(8,128)(2,1)S(1)}, u32[]{:S(2)}, u32[]{:S(2)}) collective-permute-start(bf16[384,512]{1,0:T(8,128)(2,1)} %get-tuple-element.49), channel_id=1, source_target_pairs={{0,3},{1,0},{2,1},{3,2},{4,7},{5,4},{6,5},{7,6},{8,11},{9,8},{10,9... | collective-permute-start | bytes 1179656 | tf_op jit(solution)/shard_map/ppermute | solution.py:54
  7.6 17.5 %collective-permute-start = (bf16[384,512]{1,0:T(8,128)(2,1)}, bf16[384,512]{1,0:T(8,128)(2,1)}, u32[]{:S(2)}, u32[]{:S(2)}) collective-permute-start(bf16[384,512]{1,0:T(8,128)(2,1)} %get-tuple-element.50), channel_id=1, source_target_pairs={{0,1},{1,2},{2,3},{3,0},{4,5},{5,6},{6,7},{7,4},{8,9},{9,10},{10,1... | collective-permute-start | bytes 1179656 | tf_op jit(solution)/shard_map/ppermute | solution.py:54
  11.5 7.0 %collective-permute-start.3 = (s32[4]{0:T(128)S(1)}, s32[4]{0:T(128)S(1)}, u32[]{:S(2)}, u32[]{:S(2)}) collective-permute-start(s32[4]{0:T(128)S(1)} %pad_add_fusion), channel_id=1, source_target_pairs={{0,3},{1,2},{2,1},{3,0},{4,7},{5,6},{6,5},{7,4},{8,11},{9,10},{10,... | collective-permute-start | bytes 56 | tf_op jit(solution)/shard_map/ppermute | solution.py:61
  19.4 1.4 %copy-start.2 = (bf16[1,384,2048]{2,1,0:T(8,128)(2,1)S(1)}, bf16[1,384,2048]{2,1,0:T(8,128)(2,1)}, u32[]{:S(2)}) copy-start(bf16[1,384,2048]{2,1,0:T(8,128)(2,1)} %param.7) | copy-start | bytes 4718596
  20.8 12.5 %copy-start.3 = (bf16[1,384,2048]{2,1,0:T(8,128)(2,1)S(1)}, bf16[1,384,2048]{2,1,0:T(8,128)(2,1)}, u32[]{:S(2)}) copy-start(bf16[1,384,2048]{2,1,0:T(8,128)(2,1)} %param.7) | copy-start | bytes 4718596
  21.8 5.8 %collective-permute-start.5 = (bf16[384,128]{1,0:T(8,128)(2,1)S(1)}, bf16[384,128]{1,0:T(8,128)(2,1)S(1)}, u32[]{:S(2)}, u32[]{:S(2)}) collective-permute-start(bf16[384,128]{1,0:T(8,128)(2,1)S(1)} %get-tuple-element.27), channel_id=1, source_target_pairs={{0,3},{1,2},{2,1},{3,0},{4,7},{5,6},{6,5},{7,4},{8,11},{9,10},{10,... | collective-permute-start | bytes 294920 | tf_op jit(solution)/shard_map/ppermute | solution.py:61
  22.1 5.5 %collective-permute-start.6 = (bf16[384,128]{1,0:T(8,128)(2,1)S(1)}, bf16[384,128]{1,0:T(8,128)(2,1)S(1)}, u32[]{:S(2)}, u32[]{:S(2)}) collective-permute-start(bf16[384,128]{1,0:T(8,128)(2,1)S(1)} %get-tuple-element.28), channel_id=1, source_target_pairs={{0,2},{1,3},{2,0},{3,1},{4,6},{5,7},{6,4},{7,5},{8,10},{9,11},{10,... | collective-permute-start | bytes 294920 | tf_op jit(solution)/shard_map/ppermute | solution.py:61
  22.3 6.2 %collective-permute-start.4 = (bf16[384,128]{1,0:T(8,128)(2,1)S(1)}, bf16[384,128]{1,0:T(8,128)(2,1)S(1)}, u32[]{:S(2)}, u32[]{:S(2)}) collective-permute-start(bf16[384,128]{1,0:T(8,128)(2,1)S(1)} %get-tuple-element.26), channel_id=1, source_target_pairs={{0,1},{1,0},{2,3},{3,2},{4,5},{5,4},{6,7},{7,6},{8,9},{9,8},{10,11... | collective-permute-start | bytes 294920 | tf_op jit(solution)/shard_map/ppermute | solution.py:61
  28.5 2.2 %copy-start.4 = (bf16[1,2048,1024]{2,1,0:T(8,128)(2,1)S(1)}, bf16[1,2048,1024]{2,1,0:T(8,128)(2,1)}, u32[]{:S(2)}) copy-start(bf16[1,2048,1024]{2,1,0:T(8,128)(2,1)} %param.9) | copy-start | bytes 12582916
  30.7 6.7 %copy-start.1 = (bf16[8,1,64,64,128]{4,3,2,1,0:T(8,128)(2,1)S(1)}, bf16[8,1,64,64,128]{4,3,2,1,0:T(8,128)(2,1)}, u32[]{:S(2)}) copy-start(bf16[8,1,64,64,128]{4,3,2,1,0:T(8,128)(2,1)} %param.11) | copy-start | bytes 25165828
  31.9 5.5 %collective-permute-start.7 = (bf16[1,144,128]{2,1,0:T(8,128)(2,1)S(1)}, bf16[1,144,128]{2,1,0:T(8,128)(2,1)S(1)}, u32[]{:S(2)}, u32[]{:S(2)}) collective-permute-start(bf16[1,144,128]{2,1,0:T(8,128)(2,1)S(1)} %bitcast.28), channel_id=1, source_target_pairs={{0,8},{4,12},{8,0},{12,4},{16,24},{20,28},{24,16},{28,20},{32,40},... | collective-permute-start | bytes 110600 | tf_op jit(solution)/shard_map/ppermute | solution.py:78
  33.4 9.9 %collective-permute-start.9 = (bf16[384,512]{1,0:T(8,128)(2,1)S(1)}, bf16[384,512]{1,0:T(8,128)(2,1)S(1)}, u32[]{:S(2)}, u32[]{:S(2)}) collective-permute-start(bf16[384,512]{1,0:T(8,128)(2,1)S(1)} %get-tuple-element.47), channel_id=1, source_target_pairs={{0,3},{1,0},{2,1},{3,2},{4,7},{5,4},{6,5},{7,6},{8,11},{9,8},{10,9... | collective-permute-start | bytes 1179656 | tf_op jit(solution)/shard_map/ppermute | solution.py:54
  34.5 8.8 %collective-permute-start.8 = (bf16[384,512]{1,0:T(8,128)(2,1)S(1)}, bf16[384,512]{1,0:T(8,128)(2,1)S(1)}, u32[]{:S(2)}, u32[]{:S(2)}) collective-permute-start(bf16[384,512]{1,0:T(8,128)(2,1)S(1)} %get-tuple-element.48), channel_id=1, source_target_pairs={{0,1},{1,2},{2,3},{3,0},{4,5},{5,6},{6,7},{7,4},{8,9},{9,10},{10,1... | collective-permute-start | bytes 1179656 | tf_op jit(solution)/shard_map/ppermute | solution.py:54
  35.0 27.4 %collective-permute-start.14 = (bf16[384,1024]{1,0:T(8,128)(2,1)S(1)}, bf16[384,1024]{1,0:T(8,128)(2,1)S(1)}, u32[]{:S(2)}, u32[]{:S(2)}) collective-permute-start(bf16[384,1024]{1,0:T(8,128)(2,1)S(1)} %get-tuple-element.45), channel_id=1, source_target_pairs={{0,3},{1,0},{2,1},{3,2},{4,7},{5,4},{6,5},{7,6},{8,11},{9,8},{10,9... | collective-permute-start | bytes 2359304 | tf_op jit(solution)/shard_map/ppermute | solution.py:54
  37.4 25.0 %collective-permute-start.13 = (bf16[384,1024]{1,0:T(8,128)(2,1)S(1)}, bf16[384,1024]{1,0:T(8,128)(2,1)S(1)}, u32[]{:S(2)}, u32[]{:S(2)}) collective-permute-start(bf16[384,1024]{1,0:T(8,128)(2,1)S(1)} %get-tuple-element.46), channel_id=1, source_target_pairs={{0,1},{1,2},{2,3},{3,0},{4,5},{5,6},{6,7},{7,4},{8,9},{9,10},{10,1... | collective-permute-start | bytes 2359304 | tf_op jit(solution)/shard_map/ppermute | solution.py:54
  43.3 4.8 %collective-permute-start.10 = (bf16[2,144,128]{2,1,0:T(8,128)(2,1)S(1)}, bf16[2,144,128]{2,1,0:T(8,128)(2,1)S(1)}, u32[]{:S(2)}, u32[]{:S(2)}) collective-permute-start(bf16[2,144,128]{2,1,0:T(8,128)(2,1)S(1)} %pad_maximum_fusion.3), channel_id=1, source_target_pairs={{0,24},{4,28},{8,16},{12,20},{16,8},{20,12},{24,0},{28,4},{32,56},... | collective-permute-start | bytes 221192 | tf_op jit(solution)/shard_map/ppermute | solution.py:78
  48.1 7.1 %collective-permute-start.11 = (bf16[4,144,128]{2,1,0:T(8,128)(2,1)S(1)}, bf16[4,144,128]{2,1,0:T(8,128)(2,1)S(1)}, u32[]{:S(2)}, u32[]{:S(2)}) collective-permute-start(bf16[4,144,128]{2,1,0:T(8,128)(2,1)S(1)} %constant_dynamic-update-slice_fusion), channel_id=1, source_target_pairs={{0,32},{4,36},{8,40},{12,44},{16,48},{20,52},{24,56},{28,60},{32,0... | collective-permute-start | bytes 442376 | tf_op jit(solution)/shard_map/ppermute | solution.py:78
  49.4 27.8 %copy-start.5 = (bf16[1,2048,1024]{2,1,0:T(8,128)(2,1)S(1)}, bf16[1,2048,1024]{2,1,0:T(8,128)(2,1)}, u32[]{:S(2)}) copy-start(bf16[1,2048,1024]{2,1,0:T(8,128)(2,1)} %param.9) | copy-start | bytes 12582916
  55.2 7.2 %collective-permute-start.12 = (bf16[8,144,128]{2,1,0:T(8,128)(2,1)S(1)}, bf16[8,144,128]{2,1,0:T(8,128)(2,1)S(1)}, u32[]{:S(2)}, u32[]{:S(2)}) collective-permute-start(bf16[8,144,128]{2,1,0:T(8,128)(2,1)S(1)} %pad_maximum_fusion.2), channel_id=1, source_target_pairs={{0,96},{4,100},{8,104},{12,108},{16,112},{20,116},{24,120},{28,124... | collective-permute-start | bytes 884744 | tf_op jit(solution)/shard_map/ppermute | solution.py:78
  62.5 30.0 %collective-permute-start.15 = (bf16[16,144,128]{2,1,0:T(8,128)(2,1)S(1)}, bf16[16,144,128]{2,1,0:T(8,128)(2,1)S(1)}, u32[]{:S(2)}, u32[]{:S(2)}) collective-permute-start(bf16[16,144,128]{2,1,0:T(8,128)(2,1)S(1)} %pad_maximum_fusion.1), channel_id=1, source_target_pairs={{0,4},{4,0},{8,12},{12,8},{16,20},{20,16},{24,28},{28,24},{32,36},... | collective-permute-start | bytes 1769480 | tf_op jit(solution)/shard_map/ppermute | solution.py:78
  73.0 12.1 %collective-permute-start.18 = (bf16[384,512]{1,0:T(8,128)(2,1)}, bf16[384,512]{1,0:T(8,128)(2,1)S(1)}, u32[]{:S(2)}, u32[]{:S(2)}) collective-permute-start(bf16[384,512]{1,0:T(8,128)(2,1)} %collective-permute-done.refs_0_), channel_id=1, source_target_pairs={{0,1},{1,2},{2,3},{3,0},{4,5},{5,6},{6,7},{7,4},{8,9},{9,10},{10,1... | collective-permute-start | bytes 1179656 | tf_op jit(solution)/shard_map/ppermute | solution.py:54
  73.0 12.1 %collective-permute-start.19 = (bf16[384,512]{1,0:T(8,128)(2,1)S(1)}, bf16[384,512]{1,0:T(8,128)(2,1)S(1)}, u32[]{:S(2)}, u32[]{:S(2)}) collective-permute-start(bf16[384,512]{1,0:T(8,128)(2,1)S(1)} %collective-permute-done.1.refs_3_), channel_id=1, source_target_pairs={{0,3},{1,0},{2,1},{3,2},{4,7},{5,4},{6,5},{7,6},{8,11},{9,8},{10,9... | collective-permute-start | bytes 1179656 | tf_op jit(solution)/shard_map/ppermute | solution.py:54
  75.7 16.8 %collective-permute-start.17 = (bf16[384,512]{1,0:T(8,128)(2,1)S(1)}, bf16[384,512]{1,0:T(8,128)(2,1)S(1)}, u32[]{:S(2)}, u32[]{:S(2)}) collective-permute-start(bf16[384,512]{1,0:T(8,128)(2,1)S(1)} %collective-permute-done.9.refs_4_), channel_id=1, source_target_pairs={{0,3},{1,0},{2,1},{3,2},{4,7},{5,4},{6,5},{7,6},{8,11},{9,8},{10,9... | collective-permute-start | bytes 1179656 | tf_op jit(solution)/shard_map/ppermute | solution.py:54
  75.7 17.8 %collective-permute-start.16 = (bf16[384,512]{1,0:T(8,128)(2,1)S(1)}, bf16[384,512]{1,0:T(8,128)(2,1)S(1)}, u32[]{:S(2)}, u32[]{:S(2)}) collective-permute-start(bf16[384,512]{1,0:T(8,128)(2,1)S(1)} %collective-permute-done.8.refs_1_), channel_id=1, source_target_pairs={{0,1},{1,2},{2,3},{3,0},{4,5},{5,6},{6,7},{7,4},{8,9},{9,10},{10,1... | collective-permute-start | bytes 1179656 | tf_op jit(solution)/shard_map/ppermute | solution.py:54

commit v2 on v1

--- a/solution.py
+++ b/solution.py
@@ -84,12 +84,32 @@
     return up.at[pl.ds(pl.multiple_of(owner * TOK, TOK), TOK), :]
 
 
-def reply_kernel(asked, tokens, *outs):
+def load_kernel(source, out, sem):
+    copy = pltpu.make_async_copy(source, out, sem)
+    copy.start()
+    copy.wait()
+
+
+def load(source):
+    return pl.pallas_call(
+        load_kernel,
+        out_shape=jax.ShapeDtypeStruct(source.shape, source.dtype),
+        in_specs=[whole(pltpu.HBM)],
+        out_specs=whole(VMEM),
+        scratch_shapes=[pltpu.SemaphoreType.DMA],
+        compiler_params=params(16),
+        cost_estimate=cost(0, 3 << 20),
+        name="load",
+    )(pltpu.with_memory_space_constraint(source, pltpu.HBM))
+
+
+def reply_kernel(near, across, tokens, *outs):
     low = lax.broadcasted_iota(jnp.int32, (TOK, BW), 1) < BH
     for i, out in enumerate(outs):
         halves = []
         for k in range(K):
-            row = lax.shift_right_logical(jnp.maximum(asked[i * K + k], 0), 3)
+            asked = (near if i < 2 else across)[(i % 2) * K + k]
+            row = lax.shift_right_logical(jnp.maximum(asked, 0), 3)
             start = pl.multiple_of(lax.shift_right_logical(row, 1) * BW, BW)
             pair = tokens[:, pl.ds(start, BW)].astype(F32)
             turned = pltpu.roll(pair, BH, 1)
@@ -97,16 +117,16 @@
         out[...] = jnp.where(low, halves[0], halves[1]).astype(BF16)
 
 
-def reply(asked, tokens):
+def reply(near, across, tokens):
     return pl.pallas_call(
         reply_kernel,
         out_shape=[jax.ShapeDtypeStruct((TOK, K * BH), BF16)] * NZ,
-        in_specs=[whole(SMEM), whole(VMEM)],
+        in_specs=[whole(SMEM), whole(SMEM), whole(VMEM)],
         out_specs=[whole(VMEM)] * NZ,
         compiler_params=params(4),
         cost_estimate=cost(0, 1 << 20),
         name="reply",
-    )(asked, tokens)
+    )(near, across, tokens)
 
 
 def pick_kernel(chosen, up, fb, own, c1, c2, c3, out, block, sem):
@@ -142,10 +162,10 @@
     return pl.pallas_call(
         pick_kernel,
         out_shape=jax.ShapeDtypeStruct((K * BH + NOTE, BW), BF16),
-        in_specs=[whole(SMEM), whole(VMEM), whole(pl.ANY)] + [whole(VMEM)] * NZ,
+        in_specs=[whole(SMEM), whole(VMEM), whole(pltpu.HBM)] + [whole(VMEM)] * NZ,
         out_specs=whole(VMEM),
         scratch_shapes=[VMEM((K, BH, BW), BF16), pltpu.SemaphoreType.DMA((K,))],
-        compiler_params=params(4),
+        compiler_params=params(40),
         cost_estimate=cost(2 * K * 128 * ROWS * BW, 2 << 20),
         name="pick",
     )(chosen, up, fb, *parts)
@@ -337,60 +357,52 @@
     return lax.dot_general(tokens, up, CONTRACT, preferred_element_type=F32)
 
 
-def near_total(up, fb, a, pieces, q):
-    part = slice(q * QUARTER, (q + 1) * QUARTER)
-    total = fb[part, :].astype(F32) + product(a[:, part], up_rows(up)[...])
-    for offset, (ref, at) in zip((3, 1), pieces):
-        tokens = ref[:, at * QUARTER : (at + 1) * QUARTER]
-        total += product(tokens, up_rows(up, offset)[...])
-    return total
-
-
-def middle_kernel(jobs, n_pieces, up, fb, a, *refs):
+def middle_kernel(jobs, n_pieces, up, fb, *refs):
     pieces, outs = refs[:n_pieces], refs[n_pieces:]
-    for (q, right, left), out in zip(jobs, outs):
-        near = [(pieces[i], at) for i, at in (right, left)]
-        out[...] = near_total(up, fb, a, near, q)
-
-
-def middle(up, fb, a, pieces, jobs):
+    for (q, parts), out in zip(jobs, outs):
+        total = fb[q * QUARTER : (q + 1) * QUARTER, :].astype(F32)
+        for piece, at, offset in parts:
+            tokens = pieces[piece][:, at * QUARTER : (at + 1) * QUARTER]
+            total += product(tokens, up_rows(up, offset)[...])
+        out[...] = total
+
+
+def middle(up, fb, pieces, jobs):
     return pl.pallas_call(
         functools.partial(middle_kernel, jobs, len(pieces)),
         out_shape=[ACC] * len(jobs),
-        in_specs=[whole(VMEM)] * (3 + len(pieces)),
+        in_specs=[whole(VMEM)] * (2 + len(pieces)),
         out_specs=[whole(VMEM)] * len(jobs),
         compiler_params=params(8),
         cost_estimate=cost(6 * TOK * QUARTER * QS * len(jobs), 4 << 20),
         name="middle",
-    )(up, fb, a, *pieces)
+    )(up, fb, *pieces)
 
 
 NSPLIT = 4
 
 
-def end_kernel(quarters, chosen, up, *refs):
-    n = len(quarters)
-    pieces, accs = refs[:n], refs[n : 2 * n]
-    out, staged, sem = refs[-3:]
+def end_kernel(chosen, up, low, high, q0, q1, q2, q3, out, staged, sem):
     wide = QS // NSPLIT
     copies = []
-    for j, (q, piece, acc) in enumerate(zip(quarters, pieces, accs)):
+    for q, acc in enumerate((q0, q1, q2, q3)):
+        piece = (low if q < 2 else high)[:, (q % 2) * QUARTER : (q % 2 + 1) * QUARTER]
         for s in range(NSPLIT):
             cols = slice(s * wide, (s + 1) * wide)
-            total = acc[:, cols] + product(piece[...], up_rows(up, 2)[:, cols])
+            total = acc[:, cols] + product(piece, up_rows(up, 2)[:, cols])
             for r in range(QUARTER // BH):
                 for c in range(wide // BW):
                     block = (q * QUARTER // BH + r) * 8 + s * (wide // BW) + c
                     cleared = (block == chosen[0]) | (block == chosen[1])
                     part = total[r * BH : (r + 1) * BH, c * BW : (c + 1) * BW]
                     staged[
-                        j, r * BH : (r + 1) * BH, s * wide + c * BW : s * wide + (c + 1) * BW
+                        q, r * BH : (r + 1) * BH, s * wide + c * BW : s * wide + (c + 1) * BW
                     ] = jnp.where(cleared, 0.0, part).astype(BF16)
             copies.append(
                 pltpu.make_async_copy(
-                    staged.at[j, :, cols],
+                    staged.at[q, :, cols],
                     out.at[q * QUARTER : (q + 1) * QUARTER, cols],
-                    sem.at[j, s],
+                    sem.at[q, s],
                 )
             )
             copies[-1].start()
@@ -398,20 +410,17 @@
         copy.wait()
 
 
-def end(chosen, up, pieces, accs, quarters, earlier):
-    n = len(quarters)
-    extra = [] if earlier is None else [earlier]
-    return pl.pallas_call(
-        functools.partial(end_kernel, quarters),
+def end(chosen, up, pieces, totals):
+    return pl.pallas_call(
+        end_kernel,
         out_shape=jax.ShapeDtypeStruct((D, QS), BF16),
-        in_specs=[whole(SMEM)] + [whole(VMEM)] * (1 + 2 * n) + [whole(pl.ANY)] * len(extra),
+        in_specs=[whole(SMEM)] + [whole(VMEM)] * 7,
         out_specs=whole(pl.ANY),
-        scratch_shapes=[VMEM((n, QUARTER, QS), BF16), pltpu.SemaphoreType.DMA((n, NSPLIT))],
-        input_output_aliases={2 + 2 * n: 0} if extra else {},
-        compiler_params=params(6),
-        cost_estimate=cost(2 * n * TOK * QUARTER * QS, 4 << 20),
+        scratch_shapes=[VMEM((4, QUARTER, QS), BF16), pltpu.SemaphoreType.DMA((4, NSPLIT))],
+        compiler_params=params(8),
+        cost_estimate=cost(2 * TOK * D * QS, 4 << 20),
         name="end",
-    )(chosen, up, *pieces, *accs, *extra)
+    )(chosen, up, *pieces, *totals)
 
 
 def after(value, *events):
@@ -444,46 +453,48 @@
     w2 = jnp.where(inside, (1.0 - decay_second) * jnp.power(decay_second, age), 0.0)
     vals = cycle_values.reshape(TOTAL, BH, BW)
 
-    first_r, first_l = a[:, :QUARTER], a[:, -QUARTER:]
-    right_0 = shift(first_r, "tensor", NZ, 1)
-    left_0 = shift(first_l, "tensor", NZ, -1)
     known = swap(chosen, 1)
-    asked = swap(known, 3)
-
-    parts = reply(asked, a)
+    across = pass_on(known, 3)
+    tokens = load(a)
+
+    parts = reply(known, across, tokens)
     replies = [pass_on(parts[i], flip) for i, flip in enumerate(FLIPS) if flip]
-    rest = after(a, parts[1], right_0, left_0)
-    right_1 = shift(rest[:, QUARTER:HALF], "tensor", NZ, 1)
-    left_1 = shift(rest[:, HALF:-QUARTER], "tensor", NZ, -1)
-
-    outgoing = pick(after(chosen, right_0, left_0), up, fb, [parts[0], *replies])
-    rest = after(a, outgoing)
-    right_2 = shift(rest[:, HALF:], "tensor", NZ, 1)
-    left_2 = shift(rest[:, :HALF], "tensor", NZ, -1)
+    low, high = after((tokens[:, :HALF], tokens[:, HALF:]), parts[0])
+    right_0 = shift(low, "tensor", NZ, 1)
+    left_0 = shift(high, "tensor", NZ, -1)
+    fb_far = pltpu.with_memory_space_constraint(fb, pltpu.HBM)
+    outgoing = pick(chosen, up, fb_far, [parts[0], *replies])
+    vals = load(after(vals, outgoing))
 
     got_1 = dp_exchange(outgoing[None], lambda x, y, c: (x, y ^ 1, c))
+    got_1 = after(got_1, vals)
+    high_n, low_n = after((high, low), outgoing)
+    rest_0 = shift(high_n, "tensor", NZ, 1)
+    rest_1 = shift(low_n, "tensor", NZ, -1)
     update = window(0, after(head, got_1), nxt, w1, w2, vals, None)
-    got_1 = after(got_1, update, right_1, left_1)
     got_2 = dp_exchange(got_1, lambda x, y, c: (x, y ^ 3, c))
+    got_2 = after(got_2, update)
     got_3 = dp_exchange(got_2, lambda x, y, c: (x ^ 1, y, c))
-    update = window(1, after(head, got_2), nxt, w1, w2, vals, update)
-    got_4 = dp_exchange(after(got_3, update), lambda x, y, c: (x ^ 3, y, c))
-    got = dp_exchange(after(got_4, right_2, left_2), lambda x, y, c: (x, y, c ^ 1))
-
-    far_0 = shift(after(right_0, got_2), "tensor", NZ, 1)
-    far_3 = shift(after(left_0, got_2), "tensor", NZ, -1)
-    far_1 = shift(right_1[:, :QUARTER], "tensor", NZ, 1)
-    far_2 = shift(left_1[:, -QUARTER:], "tensor", NZ, -1)
-
+    far_0 = shift(after(right_0, left_0), "tensor", NZ, 1)
+    far_1 = shift(after(left_0, right_0), "tensor", NZ, -1)
+    got_3 = after(got_3, right_0, left_0)
+    update = window(1, after(head, got_3), nxt, w1, w2, vals, update)
+    got_4 = dp_exchange(got_3, lambda x, y, c: (x ^ 3, y, c))
+    got = dp_exchange(after(got_4, update, rest_0, rest_1), lambda x, y, c: (x, y, c ^ 1))
+
+    near = [tokens, right_0, left_0, rest_0, rest_1]
+    totals = middle(
+        up,
+        fb,
+        near,
+        tuple(
+            (q, ((0, q, 0), (1, q, 3), (4, q, 1)) if q < 2 else ((0, q, 0), (3, q - 2, 3), (2, q - 2, 1)))
+            for q in range(4)
+        ),
+    )
     update_dir, newest_values = newest(head, nxt, w1, w2, got, vals, update)
-
-    near = [right_0, right_1, right_2, left_0, left_1, left_2]
-    q1, q2 = middle(up, fb, a, near, ((1, (1, 0), (5, 1)), (2, (2, 0), (4, 0))))
-    q0, q3 = middle(
-        up, fb, after(a, far_0, far_3), near, ((0, (0, 0), (5, 0)), (3, (2, 1), (3, 0)))
-    )
-    merged = end(chosen, up, [far_0, far_3], [q0, q3], (0, 3), None)
-    merged = end(chosen, up, [far_1, far_2], [q1, q2], (1, 2), merged)
+    ready = after(chosen, newest_values)
+    merged = end(ready, up, [far_0, far_1], totals)
     return (update_dir, merged[None], newest_values[None])
 
 

time: 106 us -> 82.8 us (0.78)
  waiting for transfers between devices: 20.3 us -> 8.9 us
  starting transfers between devices: 36 us -> 29.7 us
  local copies, waits for them, and re-layouts: 6.79 us -> 1.36 us
  other arithmetic: 3.53 us -> 2.14 us
  Pallas kernels: 37.3 us -> 38.6 us
    ppermute x5, waiting for transfers between devices: 7.68 us -> 2.71 us  [pass_on(): return lax.ppermute(x, 'tensor', [(i, i ^ flip) for i in range(NZ)])]
    ppermute x5, starting transfers between devices: 17.1 us -> 13.3 us  [dp_exchange(): return jnp.concatenate([value, lax.ppermute(value, 'dp', pairs)])]
    pallas_call x2 -> x3, Pallas kernels: 5.72 us -> 9.08 us  [the longest x2 4.81 us: load(): pl.pallas_call(load_kernel, out_shape=jax.ShapeDtypeStruct(source.shape,...]
    ppermute x5, waiting for transfers between devices: 8.06 us -> 4.7 us  [dp_exchange(): return jnp.concatenate([value, lax.ppermute(value, 'dp', pairs)])]
    unnamed x16 -> x7, local copies, waits for them, and re-layouts: 4.15 us -> 0.98 us
    ppermute x10 -> x6, waiting for transfers between devices: 4.51 us -> 1.48 us  [shift(): return lax.ppermute(x, axis, [(i, (i + step) % size) for i in range(size)])]
    slice x3 -> x1, local copies, waits for them, and re-layouts: 2.39 us -> 0.14 us  [local(): low, high = after((tokens[:, :HALF], tokens[:, HALF:]), parts[0])]
    ppermute x10 -> x6, starting transfers between devices: 10.3 us -> 8.1 us  [shift(): return lax.ppermute(x, axis, [(i, (i + step) % size) for i in range(size)])]
  transfers between devices with their start and end apart: 20 -> 16, of which waited for: 7 -> 5; matrix products, arithmetic and copies ran while one was open for 6% -> 4% of each run, Pallas kernels for 23% -> 41%
where the time goes in v2:
time: 82.8 us; the launch traced here: 82.4 us
  Pallas kernels  38.6 us (47%)
  starting transfers between devices  29.7 us (36%)
  waiting for transfers between devices  8.9 us (11%)
  other arithmetic  2.14 us (3%)
  between operations  1.66 us (2%)
  local copies, waits for them, and re-layouts  1.36 us (2%)
    ppermute x5, starting transfers between devices, dp_exchange(): return jnp.concatenate([value, lax.ppermute(value, 'dp', pairs)])  13.3 us
    pallas_call x2, Pallas kernels, window(): pl.pallas_call(functools.partial(window_kernel, base), out_shape=jax.Shap...  11.5 us
    pallas_call x1, Pallas kernels, newest(): pl.pallas_call(newest_kernel, out_shape=(jax.ShapeDtypeStruct((D, QS), BF...  8.67 us
    ppermute x5, starting transfers between devices, pass_on(): return lax.ppermute(x, 'tensor', [(i, i ^ flip) for i in range(NZ)])  8.3 us
    ppermute x6, starting transfers between devices, shift(): return lax.ppermute(x, axis, [(i, (i + step) % size) for i in range(size)])  8.1 us
    pallas_call x1, Pallas kernels, middle(): pl.pallas_call(functools.partial(middle_kernel, jobs, len(pieces)), out_s...  6.73 us
    pallas_call x2, Pallas kernels, load(): pl.pallas_call(load_kernel, out_shape=jax.ShapeDtypeStruct(source.shape,...  4.81 us
    ppermute x5, waiting for transfers between devices, dp_exchange(): return jnp.concatenate([value, lax.ppermute(value, 'dp', pairs)])  4.7 us
  transfers between devices with their start and end apart: 16, of which 5 were waited for; matrix products, arithmetic and copies ran while one was open for 4% of the time, Pallas kernels for 41%

profile of v2, /device:TPU:1, one launch (start us, length us, event | category | flops | bytes accessed | tf_op | source)
XLA Modules:
  0.0 82.4 jit_solution(9617032333059196412)
XLA Ops:
  0.6 2.5 %collective-permute-start = (s32[2]{0:T(128)}, s32[2]{0:T(128)S(1)}, u32[]{:S(2)}, u32[]{:S(2)}) collective-permute-start(s32[2]{0:T(128)} %bitcast.18), channel_id=1, source_target_pairs={{0,1},{1,0},{2,3},{3,2},{4,5},{5,4},{6,7},{7,6},{8,9},{9,8},{10,11... | collective-permute-start | bytes 32 | tf_op jit(solution)/shard_map/ppermute | solution.py:61
  3.8 0.1 broadcast_in_dim.58
  3.9 0.1 broadcast_in_dim.59
  4.0 0.5 broadcast.62
  4.5 1.3 %reduce.3 = s32[8,64]{1,0:T(8,128)S(1)} reduce(s32[8,1,64]{2,1,0:T(1,128)} %param.12, s32[]{:T(128)} %broadcast.62), dimensions={1}, to_apply=%param.12.reduce_sub_computation.3 | reduce | bytes 4100 | tf_op args[5]
  5.9 0.1 reshape.32
  5.9 1.4 %load.2.tokens.refs_0_ = bf16[384,2048]{1,0:T(8,128)(2,1)S(1)} custom-call(bf16[384,2048]{1,0:T(8,128)(2,1)} %bitcast.24), custom_call_target="tpu_custom_call" | custom-call | flops 1 | bytes 1 | tf_op jit(solution)/shard_map/load/pallas_call | solution.py:94
  7.4 0.0 copy-start.2
  7.4 0.0 copy-start
  7.4 0.1 fusion.3
  7.6 0.0 collective-permute-done
  7.6 0.5 copy-done.2
  8.0 0.1 pad_add_fusion.near
  8.1 2.2 %collective-permute-start.1 = (s32[4]{0:T(128)S(1)}, s32[4]{0:T(128)S(1)}, u32[]{:S(2)}, u32[]{:S(2)}) collective-permute-start(s32[4]{0:T(128)S(1)} %pad_add_fusion.near), channel_id=1, source_target_pairs={{0,3},{1,2},{2,1},{3,0},{4,7},{5,6},{6,5},{7,4},{8,11},{9,10},{10,... | collective-permute-start | bytes 56 | tf_op jit(solution)/shard_map/ppermute | solution.py:61
  10.3 1.4 %collective-permute-done.1.across = s32[4]{0:T(128)S(1)} collective-permute-done((s32[4]{0:T(128)S(1)}, s32[4]{0:T(128)S(1)}, u32[]{:S(2)}, u32[]{:S(2)}) %collective-permute-start.1) | collective-permute-done | bytes 48 | tf_op jit(solution)/shard_map/ppermute | solution.py:61
  11.7 1.0 %reply.1 = (bf16[384,128]{1,0:T(8,128)(2,1)S(1)}, bf16[384,128]{1,0:T(8,128)(2,1)S(1)}, bf16[384,128]{1,0:T(8,128)(2,1)S(1)}, bf16[384,128]{1,0:T(8,128)(2,1)S(1)}) custom-call(s32[4]{0:T(128)S(1)} %pad_add_fusion.near, s32[4]{0:T(128)S(1)} %collective-permute-done.1.across, bf16[384,2048]{1,0:T(8,128)(2,1)S(1)} %load.2.tokens.refs_0_), custom_call_target="tpu_custom_call" | custom-call | flops 1 | bytes 1 | tf_op jit(solution)/shard_map/reply/pallas_call | solution.py:121
  12.7 0.4 collective-permute-start.2
  13.1 2.1 %collective-permute-start.3 = (bf16[384,128]{1,0:T(8,128)(2,1)S(1)}, bf16[384,128]{1,0:T(8,128)(2,1)S(1)}, u32[]{:S(2)}, u32[]{:S(2)}) collective-permute-start(bf16[384,128]{1,0:T(8,128)(2,1)S(1)} %get-tuple-element.29), channel_id=1, source_target_pairs={{0,3},{1,2},{2,1},{3,0},{4,7},{5,6},{6,5},{7,4},{8,11},{9,10},{10,... | collective-permute-start | bytes 294920 | tf_op jit(solution)/shard_map/ppermute | solution.py:61
  15.1 1.1 %collective-permute-start.4 = (bf16[384,128]{1,0:T(8,128)(2,1)S(1)}, bf16[384,128]{1,0:T(8,128)(2,1)S(1)}, u32[]{:S(2)}, u32[]{:S(2)}) collective-permute-start(bf16[384,128]{1,0:T(8,128)(2,1)S(1)} %get-tuple-element.30), channel_id=1, source_target_pairs={{0,2},{1,3},{2,0},{3,1},{4,6},{5,7},{6,4},{7,5},{8,10},{9,11},{10,... | collective-permute-start | bytes 294920 | tf_op jit(solution)/shard_map/ppermute | solution.py:61
  16.2 0.1 collective-permute-start.8
  16.3 2.5 %collective-permute-start.9 = (bf16[384,1024]{1,0:T(8,128)(2,1)S(1)}, bf16[384,1024]{1,0:T(8,128)(2,1)S(1)}, u32[]{:S(2)}, u32[]{:S(2)}) collective-permute-start(bf16[384,1024]{1,0:T(8,128)(2,1)S(1)} %get-tuple-element.39), channel_id=1, source_target_pairs={{0,3},{1,0},{2,1},{3,2},{4,7},{5,4},{6,5},{7,6},{8,11},{9,8},{10,9... | collective-permute-start | bytes 2359304 | tf_op jit(solution)/shard_map/ppermute | solution.py:54
  18.9 0.3 select_reduce_fusion.nxt.old_nxt
  19.2 0.0 collective-permute-done.2.c1
  19.2 0.0 collective-permute-done.3.c2
  19.2 1.3 %collective-permute-done.4.c3 = bf16[384,128]{1,0:T(8,128)(2,1)S(1)} collective-permute-done((bf16[384,128]{1,0:T(8,128)(2,1)S(1)}, bf16[384,128]{1,0:T(8,128)(2,1)S(1)}, u32[]{:S(2)}, u32[]{:S(2)}) %collective-permute-start.4) | collective-permute-done | bytes 98336 | tf_op jit(solution)/shard_map/ppermute | solution.py:61
  20.6 0.0 copy-done
  20.6 1.7 %pick.1 = bf16[144,128]{1,0:T(8,128)(2,1)S(1)} custom-call(s32[2]{0:T(128)S(1)} %bitcast.20, bf16[1536,1024]{1,0:T(8,128)(2,1)S(1)} %bitcast.11, bf16[2048,1024]{1,0:T(8,128)(2,1)} %bitcast.14, bf16[384,128]{1,0:T(8,128)(2,1)S(1)} %get-tuple-element.27.own, bf16[384,128]{1,0:T(8,128)(2,1)S(1)} %collective-permute-done.2.c1, ...), custom_call_target="tpu_custom_call" | custom-call | flops 1 | bytes 1 | tf_op jit(solution)/shard_map/pick/pallas_call | solution.py:162
  22.3 1.4 %collective-permute-start.5 = (bf16[1,144,128]{2,1,0:T(8,128)(2,1)S(1)}, bf16[1,144,128]{2,1,0:T(8,128)(2,1)S(1)}, u32[]{:S(2)}, u32[]{:S(2)}) collective-permute-start(bf16[1,144,128]{2,1,0:T(8,128)(2,1)S(1)} %bitcast.16), channel_id=1, source_target_pairs={{0,8},{4,12},{8,0},{12,4},{16,24},{20,28},{24,16},{28,20},{32,40},... | collective-permute-start | bytes 110600 | tf_op jit(solution)/shard_map/ppermute | solution.py:78
  23.7 0.1 select_reduce_fusion.1.head
  23.8 3.4 %load.3.vals = bf16[512,64,128]{2,1,0:T(8,128)(2,1)S(1)} custom-call(bf16[512,64,128]{2,1,0:T(8,128)(2,1)} %bitcast.22), custom_call_target="tpu_custom_call" | custom-call | flops 1 | bytes 1 | tf_op jit(solution)/shard_map/load/pallas_call | solution.py:94
  27.2 0.0 collective-permute-done.5
  27.3 2.0 %collective-permute-start.6 = (bf16[2,144,128]{2,1,0:T(8,128)(2,1)S(1)}, bf16[2,144,128]{2,1,0:T(8,128)(2,1)S(1)}, u32[]{:S(2)}, u32[]{:S(2)}) collective-permute-start(bf16[2,144,128]{2,1,0:T(8,128)(2,1)S(1)} %pad_maximum_fusion.4), channel_id=1, source_target_pairs={{0,24},{4,28},{8,16},{12,20},{16,8},{20,12},{24,0},{28,4},{32,56},... | collective-permute-start | bytes 221192 | tf_op jit(solution)/shard_map/ppermute | solution.py:78
  29.3 0.9 %collective-permute-start.11 = (bf16[384,1024]{1,0:T(8,128)(2,1)S(1)}, bf16[384,1024]{1,0:T(8,128)(2,1)S(1)}, u32[]{:S(2)}, u32[]{:S(2)}) collective-permute-start(bf16[384,1024]{1,0:T(8,128)(2,1)S(1)} %get-tuple-element.39), channel_id=1, source_target_pairs={{0,1},{1,2},{2,3},{3,0},{4,5},{5,6},{6,7},{7,4},{8,9},{9,10},{10,1... | collective-permute-start | bytes 2359304 | tf_op jit(solution)/shard_map/ppermute | solution.py:54
  30.1 1.9 %collective-permute-start.12 = (bf16[384,1024]{1,0:T(8,128)(2,1)S(1)}, bf16[384,1024]{1,0:T(8,128)(2,1)S(1)}, u32[]{:S(2)}, u32[]{:S(2)}) collective-permute-start(bf16[384,1024]{1,0:T(8,128)(2,1)S(1)} %get-tuple-element.40), channel_id=1, source_target_pairs={{0,3},{1,0},{2,1},{3,2},{4,7},{5,4},{6,5},{7,6},{8,11},{9,8},{10,9... | collective-permute-start | bytes 2359304 | tf_op jit(solution)/shard_map/ppermute | solution.py:54
  32.0 5.8 %window.2.refs_0_ = bf16[2048,1024]{1,0:T(8,128)(2,1)} custom-call(s32[256]{0:T(256)S(1)} %select_reduce_fusion.1.head, s32[640]{0:T(1024)S(1)} %select_reduce_fusion.nxt.old_nxt, f32[16]{0:T(128)S(1)} %get-tuple-element.54.w1, f32[16]{0:T(128)S(1)} %get-tuple-element.53.w2, bf16[512,64,128]{2,1,0:T(8,128)(2,1)S(1)} %load.3.vals), custom_call_target="tpu_custom_call" | custom-call | flops 1 | bytes 1 | tf_op jit(solution)/shard_map/window/pallas_call | solution.py:223
  37.8 0.0 collective-permute-done.6
  37.9 1.3 %collective-permute-start.7 = (bf16[4,144,128]{2,1,0:T(8,128)(2,1)S(1)}, bf16[4,144,128]{2,1,0:T(8,128)(2,1)S(1)}, u32[]{:S(2)}, u32[]{:S(2)}) collective-permute-start(bf16[4,144,128]{2,1,0:T(8,128)(2,1)S(1)} %pad_maximum_fusion.3), channel_id=1, source_target_pairs={{0,32},{4,36},{8,40},{12,44},{16,48},{20,52},{24,56},{28,60},{32,0... | collective-permute-start | bytes 442376 | tf_op jit(solution)/shard_map/ppermute | solution.py:78
  39.2 3.1 %collective-permute-done.7 = bf16[4,144,128]{2,1,0:T(8,128)(2,1)S(1)} collective-permute-done((bf16[4,144,128]{2,1,0:T(8,128)(2,1)S(1)}, bf16[4,144,128]{2,1,0:T(8,128)(2,1)S(1)}, u32[]{:S(2)}, u32[]{:S(2)}) %collective-permute-start.7) | collective-permute-done | bytes 147488 | tf_op jit(solution)/shard_map/ppermute | solution.py:78
  42.3 0.0 collective-permute-done.8.refs_1_
  42.3 0.0 collective-permute-done.9.refs_2_
  42.3 2.6 %collective-permute-start.10 = (bf16[8,144,128]{2,1,0:T(8,128)(2,1)S(1)}, bf16[8,144,128]{2,1,0:T(8,128)(2,1)S(1)}, u32[]{:S(2)}, u32[]{:S(2)}) collective-permute-start(bf16[8,144,128]{2,1,0:T(8,128)(2,1)S(1)} %pad_maximum_fusion.2), channel_id=1, source_target_pairs={{0,96},{4,100},{8,104},{12,108},{16,112},{20,116},{24,120},{28,124... | collective-permute-start | bytes 884744 | tf_op jit(solution)/shard_map/ppermute | solution.py:78
  44.8 0.0 copy-start.1
  44.8 5.6 %window.3.update = bf16[2048,1024]{1,0:T(8,128)(2,1)} custom-call(s32[256]{0:T(256)S(1)} %select_reduce_fusion.1.head, s32[640]{0:T(1024)S(1)} %select_reduce_fusion.nxt.old_nxt, f32[16]{0:T(128)S(1)} %get-tuple-element.54.w1, f32[16]{0:T(128)S(1)} %get-tuple-element.53.w2, bf16[512,64,128]{2,1,0:T(8,128)(2,1)S(1)} %load.3.vals, ...), custom_call_target="tpu_custom_call", output_to_operand_aliasing={{}: (5, {})} | custom-call | flops 1 | bytes 1 | tf_op jit(solution)/shard_map/window/pallas_call | solution.py:223
  50.5 0.0 collective-permute-start.14
  50.5 2.7 %collective-permute-start.15 = (bf16[384,1024]{1,0:T(8,128)(2,1)S(1)}, bf16[384,1024]{1,0:T(8,128)(2,1)S(1)}, u32[]{:S(2)}, u32[]{:S(2)}) collective-permute-start(bf16[384,1024]{1,0:T(8,128)(2,1)S(1)} %collective-permute-done.9.refs_2_), channel_id=1, source_target_pairs={{0,3},{1,0},{2,1},{3,2},{4,7},{5,4},{6,5},{7,6},{8,11},{9,8},{10,9... | collective-permute-start | bytes 2359304 | tf_op jit(solution)/shard_map/ppermute | solution.py:54
  53.1 0.0 collective-permute-done.10
  53.1 0.1 pad_maximum_fusion.1
  53.2 1.5 %collective-permute-done.11.refs_3_ = bf16[384,1024]{1,0:T(8,128)(2,1)S(1)} collective-permute-done((bf16[384,1024]{1,0:T(8,128)(2,1)S(1)}, bf16[384,1024]{1,0:T(8,128)(2,1)S(1)}, u32[]{:S(2)}, u32[]{:S(2)}) %collective-permute-start.11) | collective-permute-done | bytes 786464 | tf_op jit(solution)/shard_map/ppermute | solution.py:54
  54.7 0.0 collective-permute-done.12.refs_4_
  54.7 6.1 %collective-permute-start.13 = (bf16[16,144,128]{2,1,0:T(8,128)(2,1)S(1)}, bf16[16,144,128]{2,1,0:T(8,128)(2,1)S(1)}, u32[]{:S(2)}, u32[]{:S(2)}) collective-permute-start(bf16[16,144,128]{2,1,0:T(8,128)(2,1)S(1)} %pad_maximum_fusion.1), channel_id=1, source_target_pairs={{0,4},{4,0},{8,12},{12,8},{16,20},{20,16},{24,28},{28,24},{32,36},... | collective-permute-start | bytes 1769480 | tf_op jit(solution)/shard_map/ppermute | solution.py:78
  60.8 1.6 %collective-permute-done.13 = bf16[16,144,128]{2,1,0:T(8,128)(2,1)S(1)} collective-permute-done((bf16[16,144,128]{2,1,0:T(8,128)(2,1)S(1)}, bf16[16,144,128]{2,1,0:T(8,128)(2,1)S(1)}, u32[]{:S(2)}, u32[]{:S(2)}) %collective-permute-start.13) | collective-permute-done | bytes 589856 | tf_op jit(solution)/shard_map/ppermute | solution.py:78
  62.4 0.1 pad_maximum_fusion.got
  62.5 0.0 copy-done.1
  62.5 6.7 %middle.1 = (f32[512,1024]{1,0:T(8,128)S(1)}, f32[512,1024]{1,0:T(8,128)S(1)}, f32[512,1024]{1,0:T(8,128)S(1)}, f32[512,1024]{1,0:T(8,128)S(1)}) custom-call(bf16[1536,1024]{1,0:T(8,128)(2,1)S(1)} %bitcast.12, bf16[2048,1024]{1,0:T(8,128)(2,1)S(1)} %bitcast.15, bf16[384,2048]{1,0:T(8,128)(2,1)S(1)} %load.2.tokens.refs_0_, ...), custom_call_target="tpu_custom_call" | custom-call | flops 1 | bytes 1 | tf_op jit(solution)/shard_map/middle/pallas_call | solution.py:371
  69.3 8.7 %newest.1 = (bf16[2048,1024]{1,0:T(8,128)(2,1)}, bf16[64,64,128]{2,1,0:T(8,128)(2,1)}) custom-call(s32[256]{0:T(256)S(1)} %select_reduce_fusion.1.head, s32[640]{0:T(1024)S(1)} %select_reduce_fusion.nxt.old_nxt, f32[16]{0:T(128)S(1)} %get-tuple-element.54.w1, f32[16]{0:T(128)S(1)} %get-tuple-element.53.w2, ...), custom_call_target="tpu_custom_call", output_to_operand_aliasing={{0}: (6, {})} | custom-call | flops 1 | bytes 1 | tf_op jit(solution)/shard_map/newest/pallas_call | solution.py:328
  77.9 0.0 collective-permute-done.14.low
  77.9 0.0 collective-permute-done.15.high
  78.0 4.3 %end.1 = bf16[2048,1024]{1,0:T(8,128)(2,1)} custom-call(s32[2]{0:T(128)S(1)} %bitcast.21, bf16[1536,1024]{1,0:T(8,128)(2,1)S(1)} %bitcast.13, bf16[384,1024]{1,0:T(8,128)(2,1)S(1)} %collective-permute-done.14.low, bf16[384,1024]{1,0:T(8,128)(2,1)S(1)} %collective-permute-done.15.high, f32[512,1024]{1,0:T(8,128)S(1)} %get-tuple-element.47.q0, ...), custom_call_target="tpu_custom_call" | custom-call | flops 1 | bytes 1 | tf_op jit(solution)/shard_map/end/pallas_call | solution.py:414
  (7 shorter events, 0.1 us)
Async XLA Ops:
  0.6 6.9 %collective-permute-start = (s32[2]{0:T(128)}, s32[2]{0:T(128)S(1)}, u32[]{:S(2)}, u32[]{:S(2)}) collective-permute-start(s32[2]{0:T(128)} %bitcast.18), channel_id=1, source_target_pairs={{0,1},{1,0},{2,3},{3,2},{4,5},{5,4},{6,7},{7,6},{8,9},{9,8},{10,11... | collective-permute-start | bytes 32 | tf_op jit(solution)/shard_map/ppermute | solution.py:61
  7.4 0.7 copy-start.2
  7.4 13.2 %copy-start = (bf16[1,1536,1024]{2,1,0:T(8,128)(2,1)S(1)}, bf16[1,1536,1024]{2,1,0:T(8,128)(2,1)}, u32[]{:S(2)}) copy-start(bf16[1,1536,1024]{2,1,0:T(8,128)(2,1)} %param.8) | copy-start | bytes 9437188
  8.1 3.6 %collective-permute-start.1 = (s32[4]{0:T(128)S(1)}, s32[4]{0:T(128)S(1)}, u32[]{:S(2)}, u32[]{:S(2)}) collective-permute-start(s32[4]{0:T(128)S(1)} %pad_add_fusion.near), channel_id=1, source_target_pairs={{0,3},{1,2},{2,1},{3,0},{4,7},{5,6},{6,5},{7,4},{8,11},{9,10},{10,... | collective-permute-start | bytes 56 | tf_op jit(solution)/shard_map/ppermute | solution.py:61
  12.7 6.5 %collective-permute-start.2 = (bf16[384,128]{1,0:T(8,128)(2,1)S(1)}, bf16[384,128]{1,0:T(8,128)(2,1)S(1)}, u32[]{:S(2)}, u32[]{:S(2)}) collective-permute-start(bf16[384,128]{1,0:T(8,128)(2,1)S(1)} %get-tuple-element.28), channel_id=1, source_target_pairs={{0,1},{1,0},{2,3},{3,2},{4,5},{5,4},{6,7},{7,6},{8,9},{9,8},{10,11... | collective-permute-start | bytes 294920 | tf_op jit(solution)/shard_map/ppermute | solution.py:61
  13.1 6.1 %collective-permute-start.3 = (bf16[384,128]{1,0:T(8,128)(2,1)S(1)}, bf16[384,128]{1,0:T(8,128)(2,1)S(1)}, u32[]{:S(2)}, u32[]{:S(2)}) collective-permute-start(bf16[384,128]{1,0:T(8,128)(2,1)S(1)} %get-tuple-element.29), channel_id=1, source_target_pairs={{0,3},{1,2},{2,1},{3,0},{4,7},{5,6},{6,5},{7,4},{8,11},{9,10},{10,... | collective-permute-start | bytes 294920 | tf_op jit(solution)/shard_map/ppermute | solution.py:61
  15.1 5.4 %collective-permute-start.4 = (bf16[384,128]{1,0:T(8,128)(2,1)S(1)}, bf16[384,128]{1,0:T(8,128)(2,1)S(1)}, u32[]{:S(2)}, u32[]{:S(2)}) collective-permute-start(bf16[384,128]{1,0:T(8,128)(2,1)S(1)} %get-tuple-element.30), channel_id=1, source_target_pairs={{0,2},{1,3},{2,0},{3,1},{4,6},{5,7},{6,4},{7,5},{8,10},{9,11},{10,... | collective-permute-start | bytes 294920 | tf_op jit(solution)/shard_map/ppermute | solution.py:61
  16.2 26.1 %collective-permute-start.8 = (bf16[384,1024]{1,0:T(8,128)(2,1)S(1)}, bf16[384,1024]{1,0:T(8,128)(2,1)S(1)}, u32[]{:S(2)}, u32[]{:S(2)}) collective-permute-start(bf16[384,1024]{1,0:T(8,128)(2,1)S(1)} %get-tuple-element.40), channel_id=1, source_target_pairs={{0,1},{1,2},{2,3},{3,0},{4,5},{5,6},{6,7},{7,4},{8,9},{9,10},{10,1... | collective-permute-start | bytes 2359304 | tf_op jit(solution)/shard_map/ppermute | solution.py:54
  16.3 25.9 %collective-permute-start.9 = (bf16[384,1024]{1,0:T(8,128)(2,1)S(1)}, bf16[384,1024]{1,0:T(8,128)(2,1)S(1)}, u32[]{:S(2)}, u32[]{:S(2)}) collective-permute-start(bf16[384,1024]{1,0:T(8,128)(2,1)S(1)} %get-tuple-element.39), channel_id=1, source_target_pairs={{0,3},{1,0},{2,1},{3,2},{4,7},{5,4},{6,5},{7,6},{8,11},{9,8},{10,9... | collective-permute-start | bytes 2359304 | tf_op jit(solution)/shard_map/ppermute | solution.py:54
  22.3 4.9 %collective-permute-start.5 = (bf16[1,144,128]{2,1,0:T(8,128)(2,1)S(1)}, bf16[1,144,128]{2,1,0:T(8,128)(2,1)S(1)}, u32[]{:S(2)}, u32[]{:S(2)}) collective-permute-start(bf16[1,144,128]{2,1,0:T(8,128)(2,1)S(1)} %bitcast.16), channel_id=1, source_target_pairs={{0,8},{4,12},{8,0},{12,4},{16,24},{20,28},{24,16},{28,20},{32,40},... | collective-permute-start | bytes 110600 | tf_op jit(solution)/shard_map/ppermute | solution.py:78
  27.3 10.6 %collective-permute-start.6 = (bf16[2,144,128]{2,1,0:T(8,128)(2,1)S(1)}, bf16[2,144,128]{2,1,0:T(8,128)(2,1)S(1)}, u32[]{:S(2)}, u32[]{:S(2)}) collective-permute-start(bf16[2,144,128]{2,1,0:T(8,128)(2,1)S(1)} %pad_maximum_fusion.4), channel_id=1, source_target_pairs={{0,24},{4,28},{8,16},{12,20},{16,8},{20,12},{24,0},{28,4},{32,56},... | collective-permute-start | bytes 221192 | tf_op jit(solution)/shard_map/ppermute | solution.py:78
  29.3 25.4 %collective-permute-start.11 = (bf16[384,1024]{1,0:T(8,128)(2,1)S(1)}, bf16[384,1024]{1,0:T(8,128)(2,1)S(1)}, u32[]{:S(2)}, u32[]{:S(2)}) collective-permute-start(bf16[384,1024]{1,0:T(8,128)(2,1)S(1)} %get-tuple-element.39), channel_id=1, source_target_pairs={{0,1},{1,2},{2,3},{3,0},{4,5},{5,6},{6,7},{7,4},{8,9},{9,10},{10,1... | collective-permute-start | bytes 2359304 | tf_op jit(solution)/shard_map/ppermute | solution.py:54
  30.1 24.5 %collective-permute-start.12 = (bf16[384,1024]{1,0:T(8,128)(2,1)S(1)}, bf16[384,1024]{1,0:T(8,128)(2,1)S(1)}, u32[]{:S(2)}, u32[]{:S(2)}) collective-permute-start(bf16[384,1024]{1,0:T(8,128)(2,1)S(1)} %get-tuple-element.40), channel_id=1, source_target_pairs={{0,3},{1,0},{2,1},{3,2},{4,7},{5,4},{6,5},{7,6},{8,11},{9,8},{10,9... | collective-permute-start | bytes 2359304 | tf_op jit(solution)/shard_map/ppermute | solution.py:54
  37.9 4.4 %collective-permute-start.7 = (bf16[4,144,128]{2,1,0:T(8,128)(2,1)S(1)}, bf16[4,144,128]{2,1,0:T(8,128)(2,1)S(1)}, u32[]{:S(2)}, u32[]{:S(2)}) collective-permute-start(bf16[4,144,128]{2,1,0:T(8,128)(2,1)S(1)} %pad_maximum_fusion.3), channel_id=1, source_target_pairs={{0,32},{4,36},{8,40},{12,44},{16,48},{20,52},{24,56},{28,60},{32,0... | collective-permute-start | bytes 442376 | tf_op jit(solution)/shard_map/ppermute | solution.py:78
  42.3 10.9 %collective-permute-start.10 = (bf16[8,144,128]{2,1,0:T(8,128)(2,1)S(1)}, bf16[8,144,128]{2,1,0:T(8,128)(2,1)S(1)}, u32[]{:S(2)}, u32[]{:S(2)}) collective-permute-start(bf16[8,144,128]{2,1,0:T(8,128)(2,1)S(1)} %pad_maximum_fusion.2), channel_id=1, source_target_pairs={{0,96},{4,100},{8,104},{12,108},{16,112},{20,116},{24,120},{28,124... | collective-permute-start | bytes 884744 | tf_op jit(solution)/shard_map/ppermute | solution.py:78
  44.8 17.7 %copy-start.1 = (bf16[1,2048,1024]{2,1,0:T(8,128)(2,1)S(1)}, bf16[1,2048,1024]{2,1,0:T(8,128)(2,1)}, u32[]{:S(2)}) copy-start(bf16[1,2048,1024]{2,1,0:T(8,128)(2,1)} %param.9) | copy-start | bytes 12582916
  50.5 27.5 %collective-permute-start.14 = (bf16[384,1024]{1,0:T(8,128)(2,1)S(1)}, bf16[384,1024]{1,0:T(8,128)(2,1)S(1)}, u32[]{:S(2)}, u32[]{:S(2)}) collective-permute-start(bf16[384,1024]{1,0:T(8,128)(2,1)S(1)} %collective-permute-done.8.refs_1_), channel_id=1, source_target_pairs={{0,1},{1,2},{2,3},{3,0},{4,5},{5,6},{6,7},{7,4},{8,9},{9,10},{10,1... | collective-permute-start | bytes 2359304 | tf_op jit(solution)/shard_map/ppermute | solution.py:54
  50.5 27.5 %collective-permute-start.15 = (bf16[384,1024]{1,0:T(8,128)(2,1)S(1)}, bf16[384,1024]{1,0:T(8,128)(2,1)S(1)}, u32[]{:S(2)}, u32[]{:S(2)}) collective-permute-start(bf16[384,1024]{1,0:T(8,128)(2,1)S(1)} %collective-permute-done.9.refs_2_), channel_id=1, source_target_pairs={{0,3},{1,0},{2,1},{3,2},{4,7},{5,4},{6,5},{7,6},{8,11},{9,8},{10,9... | collective-permute-start | bytes 2359304 | tf_op jit(solution)/shard_map/ppermute | solution.py:54
  54.7 7.7 %collective-permute-start.13 = (bf16[16,144,128]{2,1,0:T(8,128)(2,1)S(1)}, bf16[16,144,128]{2,1,0:T(8,128)(2,1)S(1)}, u32[]{:S(2)}, u32[]{:S(2)}) collective-permute-start(bf16[16,144,128]{2,1,0:T(8,128)(2,1)S(1)} %pad_maximum_fusion.1), channel_id=1, source_target_pairs={{0,4},{4,0},{8,12},{12,8},{16,20},{20,16},{24,28},{28,24},{32,36},... | collective-permute-start | bytes 1769480 | tf_op jit(solution)/shard_map/ppermute | solution.py:78

commit v3 on v2

--- a/solution.py
+++ b/solution.py
@@ -69,13 +69,14 @@
     return (x * NY + y) * NC + c
 
 
-def dp_exchange(value, partner):
+def dp_exchange(value, partner, meanwhile=()):
     pairs = []
     for x in range(NX):
         for y in range(NY):
             for c in range(NC):
                 pairs.append((dp_index(x, y, c), dp_index(*partner(x, y, c))))
-    return jnp.concatenate([value, lax.ppermute(value, "dp", pairs)])
+    received = lax.ppermute(value, "dp", pairs)
+    return jnp.concatenate([value, lax.optimization_barrier((received, meanwhile))[0]])
 
 
 def up_rows(up, offset=0, flip=0):
@@ -357,29 +358,48 @@
     return lax.dot_general(tokens, up, CONTRACT, preferred_element_type=F32)
 
 
-def middle_kernel(jobs, n_pieces, up, fb, *refs):
-    pieces, outs = refs[:n_pieces], refs[n_pieces:]
-    for (q, parts), out in zip(jobs, outs):
-        total = fb[q * QUARTER : (q + 1) * QUARTER, :].astype(F32)
-        for piece, at, offset in parts:
-            tokens = pieces[piece][:, at * QUARTER : (at + 1) * QUARTER]
-            total += product(tokens, up_rows(up, offset)[...])
-        out[...] = total
-
-
-def middle(up, fb, pieces, jobs):
-    return pl.pallas_call(
-        functools.partial(middle_kernel, jobs, len(pieces)),
-        out_shape=[ACC] * len(jobs),
-        in_specs=[whole(VMEM)] * (2 + len(pieces)),
-        out_specs=[whole(VMEM)] * len(jobs),
+def first_kernel(up, fb, tokens, right, left, *outs):
+    for q, out in enumerate(outs):
+        part = slice(q * QUARTER, (q + 1) * QUARTER)
+        total = fb[part, :].astype(F32) + product(tokens[:, part], up_rows(up)[...])
+        piece, offset = (right, 3) if q < 2 else (left, 1)
+        half = slice((q % 2) * QUARTER, (q % 2 + 1) * QUARTER)
+        out[...] = total + product(piece[:, half], up_rows(up, offset)[...])
+
+
+def first_products(up, fb, tokens, right, left):
+    return pl.pallas_call(
+        first_kernel,
+        out_shape=[ACC] * 4,
+        in_specs=[whole(VMEM)] * 5,
+        out_specs=[whole(VMEM)] * 4,
         compiler_params=params(8),
-        cost_estimate=cost(6 * TOK * QUARTER * QS * len(jobs), 4 << 20),
-        name="middle",
-    )(up, fb, *pieces)
-
-
-NSPLIT = 4
+        cost_estimate=cost(4 * TOK * D * QS, 4 << 20),
+        name="first_products",
+    )(up, fb, tokens, right, left)
+
+
+def second_kernel(up, right, left, q0, q1, q2, q3, *outs):
+    for q, (acc, out) in enumerate(zip((q0, q1, q2, q3), outs)):
+        piece, offset = (left, 1) if q < 2 else (right, 3)
+        half = slice((q % 2) * QUARTER, (q % 2 + 1) * QUARTER)
+        out[...] = acc[...] + product(piece[:, half], up_rows(up, offset)[...])
+
+
+def second_products(up, right, left, totals):
+    return pl.pallas_call(
+        second_kernel,
+        out_shape=[ACC] * 4,
+        in_specs=[whole(VMEM)] * 7,
+        out_specs=[whole(VMEM)] * 4,
+        input_output_aliases={3 + i: i for i in range(4)},
+        compiler_params=params(8),
+        cost_estimate=cost(2 * TOK * D * QS, 4 << 20),
+        name="second_products",
+    )(up, right, left, *totals)
+
+
+NSPLIT = 2
 
 
 def end_kernel(chosen, up, low, high, q0, q1, q2, q3, out, staged, sem):
@@ -465,33 +485,20 @@
     fb_far = pltpu.with_memory_space_constraint(fb, pltpu.HBM)
     outgoing = pick(chosen, up, fb_far, [parts[0], *replies])
     vals = load(after(vals, outgoing))
-
-    got_1 = dp_exchange(outgoing[None], lambda x, y, c: (x, y ^ 1, c))
-    got_1 = after(got_1, vals)
+    got_1 = dp_exchange(outgoing[None], lambda x, y, c: (x, y ^ 1, c), vals)
     high_n, low_n = after((high, low), outgoing)
     rest_0 = shift(high_n, "tensor", NZ, 1)
     rest_1 = shift(low_n, "tensor", NZ, -1)
     update = window(0, after(head, got_1), nxt, w1, w2, vals, None)
-    got_2 = dp_exchange(got_1, lambda x, y, c: (x, y ^ 3, c))
-    got_2 = after(got_2, update)
-    got_3 = dp_exchange(got_2, lambda x, y, c: (x ^ 1, y, c))
+    got_2 = dp_exchange(got_1, lambda x, y, c: (x, y ^ 3, c), update)
+    totals = first_products(up, after(fb, got_2), tokens, right_0, left_0)
+    got_3 = dp_exchange(got_2, lambda x, y, c: (x ^ 1, y, c), totals)
     far_0 = shift(after(right_0, left_0), "tensor", NZ, 1)
     far_1 = shift(after(left_0, right_0), "tensor", NZ, -1)
-    got_3 = after(got_3, right_0, left_0)
     update = window(1, after(head, got_3), nxt, w1, w2, vals, update)
-    got_4 = dp_exchange(got_3, lambda x, y, c: (x ^ 3, y, c))
-    got = dp_exchange(after(got_4, update, rest_0, rest_1), lambda x, y, c: (x, y, c ^ 1))
-
-    near = [tokens, right_0, left_0, rest_0, rest_1]
-    totals = middle(
-        up,
-        fb,
-        near,
-        tuple(
-            (q, ((0, q, 0), (1, q, 3), (4, q, 1)) if q < 2 else ((0, q, 0), (3, q - 2, 3), (2, q - 2, 1)))
-            for q in range(4)
-        ),
-    )
+    got_4 = dp_exchange(got_3, lambda x, y, c: (x ^ 3, y, c), (update, rest_0, rest_1))
+    totals = second_products(up, after(rest_0, got_4), rest_1, totals)
+    got = dp_exchange(got_4, lambda x, y, c: (x, y, c ^ 1), totals)
     update_dir, newest_values = newest(head, nxt, w1, w2, got, vals, update)
     ready = after(chosen, newest_values)
     merged = end(ready, up, [far_0, far_1], totals)

time: 82.8 us -> 77.6 us (0.937)
  waiting for transfers between devices: 8.9 us -> 2.98 us
    ppermute x5, waiting for transfers between devices: 4.7 us -> 0.01 us  [dp_exchange(): received = lax.ppermute(value, 'dp', pairs)]
    ppermute x6, waiting for transfers between devices: 1.48 us -> 0.26 us  [shift(): return lax.ppermute(x, axis, [(i, (i + step) % size) for i in range(size)])]
    pallas_call x1 -> x2, Pallas kernels: 6.73 us -> 7.38 us  [the longest x1 4.57 us: first_products(): pl.pallas_call(first_kernel, out_shape=[ACC] * 4, in_specs=[whole(VMEM)]...]
  transfers between devices with their start and end apart: 16 -> 16, of which waited for: 5 -> 3; matrix products, arithmetic and copies ran while one was open for 4% -> 4% of each run, Pallas kernels for 41% -> 44%
where the time goes in v3:
time: 77.6 us; the launch traced here: 77.3 us
  Pallas kernels  39.2 us (51%)
  starting transfers between devices  29.8 us (38%)
  waiting for transfers between devices  2.98 us (4%)
  other arithmetic  1.99 us (3%)
  between operations  1.7 us (2%)
  local copies, waits for them, and re-layouts  1.66 us (2%)
    ppermute x5, starting transfers between devices, dp_exchange(): received = lax.ppermute(value, 'dp', pairs)  13.3 us
    pallas_call x2, Pallas kernels, window(): pl.pallas_call(functools.partial(window_kernel, base), out_shape=jax.Shap...  11.7 us
    pallas_call x1, Pallas kernels, newest(): pl.pallas_call(newest_kernel, out_shape=(jax.ShapeDtypeStruct((D, QS), BF...  8.81 us
    ppermute x5, starting transfers between devices, pass_on(): return lax.ppermute(x, 'tensor', [(i, i ^ flip) for i in range(NZ)])  8.3 us
    ppermute x6, starting transfers between devices, shift(): return lax.ppermute(x, axis, [(i, (i + step) % size) for i in range(size)])  8.16 us
    pallas_call x2, Pallas kernels, load(): pl.pallas_call(load_kernel, out_shape=jax.ShapeDtypeStruct(source.shape,...  4.81 us
    pallas_call x1, Pallas kernels, first_products(): pl.pallas_call(first_kernel, out_shape=[ACC] * 4, in_specs=[whole(VMEM)]...  4.57 us
    pallas_call x1, Pallas kernels, end(): pl.pallas_call(end_kernel, out_shape=jax.ShapeDtypeStruct((D, QS), BF16),...  3.84 us
  transfers between devices with their start and end apart: 16, of which 3 were waited for; matrix products, arithmetic and copies ran while one was open for 4% of the time, Pallas kernels for 44%

profile of v3, /device:TPU:1, one launch (start us, length us, event | category | flops | bytes accessed | tf_op | source)
XLA Modules:
  0.0 77.3 jit_solution(11014303620904488133)
XLA Ops:
  0.6 2.5 %collective-permute-start = (s32[2]{0:T(128)}, s32[2]{0:T(128)S(1)}, u32[]{:S(2)}, u32[]{:S(2)}) collective-permute-start(s32[2]{0:T(128)} %bitcast.23), channel_id=1, source_target_pairs={{0,1},{1,0},{2,3},{3,2},{4,5},{5,4},{6,7},{7,6},{8,9},{9,8},{10,11... | collective-permute-start | bytes 32 | tf_op jit(solution)/shard_map/ppermute | solution.py:61
  3.8 0.1 broadcast_in_dim.58
  3.9 0.1 broadcast_in_dim.59
  4.0 0.5 broadcast.62
  4.5 1.3 %reduce.3 = s32[8,64]{1,0:T(8,128)S(1)} reduce(s32[8,1,64]{2,1,0:T(1,128)} %param.12, s32[]{:T(128)} %broadcast.62), dimensions={1}, to_apply=%param.12.reduce_sub_computation.3 | reduce | bytes 4100 | tf_op args[5]
  5.9 0.1 reshape.32
  5.9 1.4 %load.2.tokens = bf16[384,2048]{1,0:T(8,128)(2,1)S(1)} custom-call(bf16[384,2048]{1,0:T(8,128)(2,1)} %bitcast.29), custom_call_target="tpu_custom_call" | custom-call | flops 1 | bytes 1 | tf_op jit(solution)/shard_map/load/pallas_call | solution.py:95
  7.4 0.0 copy-start.2
  7.4 0.0 copy-start
  7.4 0.1 fusion.3
  7.6 0.0 collective-permute-done
  7.6 0.5 copy-done.2
  8.0 0.1 pad_add_fusion.near
  8.1 2.2 %collective-permute-start.1 = (s32[4]{0:T(128)S(1)}, s32[4]{0:T(128)S(1)}, u32[]{:S(2)}, u32[]{:S(2)}) collective-permute-start(s32[4]{0:T(128)S(1)} %pad_add_fusion.near), channel_id=1, source_target_pairs={{0,3},{1,2},{2,1},{3,0},{4,7},{5,6},{6,5},{7,4},{8,11},{9,10},{10,... | collective-permute-start | bytes 56 | tf_op jit(solution)/shard_map/ppermute | solution.py:61
  10.3 1.4 %collective-permute-done.1.across = s32[4]{0:T(128)S(1)} collective-permute-done((s32[4]{0:T(128)S(1)}, s32[4]{0:T(128)S(1)}, u32[]{:S(2)}, u32[]{:S(2)}) %collective-permute-start.1) | collective-permute-done | bytes 48 | tf_op jit(solution)/shard_map/ppermute | solution.py:61
  11.7 1.0 %reply.1 = (bf16[384,128]{1,0:T(8,128)(2,1)S(1)}, bf16[384,128]{1,0:T(8,128)(2,1)S(1)}, bf16[384,128]{1,0:T(8,128)(2,1)S(1)}, bf16[384,128]{1,0:T(8,128)(2,1)S(1)}) custom-call(s32[4]{0:T(128)S(1)} %pad_add_fusion.near, s32[4]{0:T(128)S(1)} %collective-permute-done.1.across, bf16[384,2048]{1,0:T(8,128)(2,1)S(1)} %load.2.tokens), custom_call_target="tpu_custom_call" | custom-call | flops 1 | bytes 1 | tf_op jit(solution)/shard_map/reply/pallas_call | solution.py:122
  12.7 0.4 collective-permute-start.2
  13.1 2.1 %collective-permute-start.3 = (bf16[384,128]{1,0:T(8,128)(2,1)S(1)}, bf16[384,128]{1,0:T(8,128)(2,1)S(1)}, u32[]{:S(2)}, u32[]{:S(2)}) collective-permute-start(bf16[384,128]{1,0:T(8,128)(2,1)S(1)} %get-tuple-element.36), channel_id=1, source_target_pairs={{0,3},{1,2},{2,1},{3,0},{4,7},{5,6},{6,5},{7,4},{8,11},{9,10},{10,... | collective-permute-start | bytes 294920 | tf_op jit(solution)/shard_map/ppermute | solution.py:61
  15.1 1.0 %collective-permute-start.4 = (bf16[384,128]{1,0:T(8,128)(2,1)S(1)}, bf16[384,128]{1,0:T(8,128)(2,1)S(1)}, u32[]{:S(2)}, u32[]{:S(2)}) collective-permute-start(bf16[384,128]{1,0:T(8,128)(2,1)S(1)} %get-tuple-element.37), channel_id=1, source_target_pairs={{0,2},{1,3},{2,0},{3,1},{4,6},{5,7},{6,4},{7,5},{8,10},{9,11},{10,... | collective-permute-start | bytes 294920 | tf_op jit(solution)/shard_map/ppermute | solution.py:61
  16.2 0.1 collective-permute-start.8
  16.3 2.5 %collective-permute-start.9 = (bf16[384,1024]{1,0:T(8,128)(2,1)S(1)}, bf16[384,1024]{1,0:T(8,128)(2,1)S(1)}, u32[]{:S(2)}, u32[]{:S(2)}) collective-permute-start(bf16[384,1024]{1,0:T(8,128)(2,1)S(1)} %get-tuple-element.51), channel_id=1, source_target_pairs={{0,3},{1,0},{2,1},{3,2},{4,7},{5,4},{6,5},{7,6},{8,11},{9,8},{10,9... | collective-permute-start | bytes 2359304 | tf_op jit(solution)/shard_map/ppermute | solution.py:54
  18.9 0.3 select_reduce_fusion.nxt.old_nxt
  19.2 0.0 collective-permute-done.2.c1
  19.2 0.0 collective-permute-done.3.c2
  19.2 1.3 %collective-permute-done.4.c3 = bf16[384,128]{1,0:T(8,128)(2,1)S(1)} collective-permute-done((bf16[384,128]{1,0:T(8,128)(2,1)S(1)}, bf16[384,128]{1,0:T(8,128)(2,1)S(1)}, u32[]{:S(2)}, u32[]{:S(2)}) %collective-permute-start.4) | collective-permute-done | bytes 98336 | tf_op jit(solution)/shard_map/ppermute | solution.py:61
  20.6 0.0 copy-done
  20.6 1.7 %pick.1 = bf16[144,128]{1,0:T(8,128)(2,1)S(1)} custom-call(s32[2]{0:T(128)S(1)} %bitcast.25, bf16[1536,1024]{1,0:T(8,128)(2,1)S(1)} %bitcast.13, bf16[2048,1024]{1,0:T(8,128)(2,1)} %bitcast.17, bf16[384,128]{1,0:T(8,128)(2,1)S(1)} %get-tuple-element.34.own, bf16[384,128]{1,0:T(8,128)(2,1)S(1)} %collective-permute-done.2.c1, ...), custom_call_target="tpu_custom_call" | custom-call | flops 1 | bytes 1 | tf_op jit(solution)/shard_map/pick/pallas_call | solution.py:163
  22.3 1.4 %collective-permute-start.5 = (bf16[1,144,128]{2,1,0:T(8,128)(2,1)S(1)}, bf16[1,144,128]{2,1,0:T(8,128)(2,1)S(1)}, u32[]{:S(2)}, u32[]{:S(2)}) collective-permute-start(bf16[1,144,128]{2,1,0:T(8,128)(2,1)S(1)} %bitcast.19), channel_id=1, source_target_pairs={{0,8},{4,12},{8,0},{12,4},{16,24},{20,28},{24,16},{28,20},{32,40},... | collective-permute-start | bytes 110600 | tf_op jit(solution)/shard_map/ppermute | solution.py:78
  23.7 0.1 select_reduce_fusion.1.head
  23.8 3.4 %load.3.vals = bf16[512,64,128]{2,1,0:T(8,128)(2,1)S(1)} custom-call(bf16[512,64,128]{2,1,0:T(8,128)(2,1)} %bitcast.27), custom_call_target="tpu_custom_call" | custom-call | flops 1 | bytes 1 | tf_op jit(solution)/shard_map/load/pallas_call | solution.py:95
  27.2 0.0 collective-permute-done.5
  27.3 2.0 %collective-permute-start.6 = (bf16[2,144,128]{2,1,0:T(8,128)(2,1)S(1)}, bf16[2,144,128]{2,1,0:T(8,128)(2,1)S(1)}, u32[]{:S(2)}, u32[]{:S(2)}) collective-permute-start(bf16[2,144,128]{2,1,0:T(8,128)(2,1)S(1)} %pad_maximum_fusion.2), channel_id=1, source_target_pairs={{0,24},{4,28},{8,16},{12,20},{16,8},{20,12},{24,0},{28,4},{32,56},... | collective-permute-start | bytes 221192 | tf_op jit(solution)/shard_map/ppermute | solution.py:78
  29.3 0.9 %collective-permute-start.11 = (bf16[384,1024]{1,0:T(8,128)(2,1)S(1)}, bf16[384,1024]{1,0:T(8,128)(2,1)S(1)}, u32[]{:S(2)}, u32[]{:S(2)}) collective-permute-start(bf16[384,1024]{1,0:T(8,128)(2,1)S(1)} %get-tuple-element.51), channel_id=1, source_target_pairs={{0,1},{1,2},{2,3},{3,0},{4,5},{5,6},{6,7},{7,4},{8,9},{9,10},{10,1... | collective-permute-start | bytes 2359304 | tf_op jit(solution)/shard_map/ppermute | solution.py:54
  30.1 1.9 %collective-permute-start.12 = (bf16[384,1024]{1,0:T(8,128)(2,1)S(1)}, bf16[384,1024]{1,0:T(8,128)(2,1)S(1)}, u32[]{:S(2)}, u32[]{:S(2)}) collective-permute-start(bf16[384,1024]{1,0:T(8,128)(2,1)S(1)} %get-tuple-element.52), channel_id=1, source_target_pairs={{0,3},{1,0},{2,1},{3,2},{4,7},{5,4},{6,5},{7,6},{8,11},{9,8},{10,9... | collective-permute-start | bytes 2359304 | tf_op jit(solution)/shard_map/ppermute | solution.py:54
  32.0 0.0 copy-start.1
  32.0 5.8 %window.2.refs_0_ = bf16[2048,1024]{1,0:T(8,128)(2,1)} custom-call(s32[256]{0:T(256)S(1)} %select_reduce_fusion.1.head, s32[640]{0:T(1024)S(1)} %select_reduce_fusion.nxt.old_nxt, f32[16]{0:T(128)S(1)} %get-tuple-element.78.w1, f32[16]{0:T(128)S(1)} %get-tuple-element.77.w2, bf16[512,64,128]{2,1,0:T(8,128)(2,1)S(1)} %load.3.vals), custom_call_target="tpu_custom_call" | custom-call | flops 1 | bytes 1 | tf_op jit(solution)/shard_map/window/pallas_call | solution.py:224
  37.8 0.0 collective-permute-done.6
  37.8 1.3 %collective-permute-start.7 = (bf16[4,144,128]{2,1,0:T(8,128)(2,1)S(1)}, bf16[4,144,128]{2,1,0:T(8,128)(2,1)S(1)}, u32[]{:S(2)}, u32[]{:S(2)}) collective-permute-start(bf16[4,144,128]{2,1,0:T(8,128)(2,1)S(1)} %pad_maximum_fusion.1), channel_id=1, source_target_pairs={{0,32},{4,36},{8,40},{12,44},{16,48},{20,52},{24,56},{28,60},{32,0... | collective-permute-start | bytes 442376 | tf_op jit(solution)/shard_map/ppermute | solution.py:78
  39.1 0.0 collective-permute-done.8.right
  39.1 0.0 collective-permute-done.9.left
  39.1 0.0 copy-done.1
  39.1 4.6 %first_products.1 = (f32[512,1024]{1,0:T(8,128)S(1)}, f32[512,1024]{1,0:T(8,128)S(1)}, f32[512,1024]{1,0:T(8,128)S(1)}, f32[512,1024]{1,0:T(8,128)S(1)}) custom-call(bf16[1536,1024]{1,0:T(8,128)(2,1)S(1)} %bitcast.14, bf16[2048,1024]{1,0:T(8,128)(2,1)S(1)} %bitcast.18, bf16[384,2048]{1,0:T(8,128)(2,1)S(1)} %load.2.tokens, ...), custom_call_target="tpu_custom_call" | custom-call | flops 1 | bytes 1 | tf_op jit(solution)/shard_map/first_products/pallas_call | solution.py:371
  43.7 0.0 collective-permute-done.7
  43.7 1.9 %collective-permute-start.10 = (bf16[8,144,128]{2,1,0:T(8,128)(2,1)S(1)}, bf16[8,144,128]{2,1,0:T(8,128)(2,1)S(1)}, u32[]{:S(2)}, u32[]{:S(2)}) collective-permute-start(bf16[8,144,128]{2,1,0:T(8,128)(2,1)S(1)} %pad_maximum_fusion), channel_id=1, source_target_pairs={{0,96},{4,100},{8,104},{12,108},{16,112},{20,116},{24,120},{28,124... | collective-permute-start | bytes 884744 | tf_op jit(solution)/shard_map/ppermute | solution.py:78
  45.7 0.1 collective-permute-start.14
  45.8 2.7 %collective-permute-start.15 = (bf16[384,1024]{1,0:T(8,128)(2,1)S(1)}, bf16[384,1024]{1,0:T(8,128)(2,1)S(1)}, u32[]{:S(2)}, u32[]{:S(2)}) collective-permute-start(bf16[384,1024]{1,0:T(8,128)(2,1)S(1)} %collective-permute-done.9.left), channel_id=1, source_target_pairs={{0,3},{1,0},{2,1},{3,2},{4,7},{5,4},{6,5},{7,6},{8,11},{9,8},{10,9... | collective-permute-start | bytes 2359304 | tf_op jit(solution)/shard_map/ppermute | solution.py:54
  48.4 5.9 %window.3.update = bf16[2048,1024]{1,0:T(8,128)(2,1)} custom-call(s32[256]{0:T(256)S(1)} %select_reduce_fusion.1.head, s32[640]{0:T(1024)S(1)} %select_reduce_fusion.nxt.old_nxt, f32[16]{0:T(128)S(1)} %get-tuple-element.78.w1, f32[16]{0:T(128)S(1)} %get-tuple-element.77.w2, bf16[512,64,128]{2,1,0:T(8,128)(2,1)S(1)} %load.3.vals, ...), custom_call_target="tpu_custom_call", output_to_operand_aliasing={{}: (5, {})} | custom-call | flops 1 | bytes 1 | tf_op jit(solution)/shard_map/window/pallas_call | solution.py:224
  54.4 0.1 constant_dynamic-update-slice_fusion.1
  54.4 0.2 collective-permute-done.11.right
  54.7 0.0 collective-permute-done.12.left
  54.7 0.0 collective-permute-done.10
  54.7 0.1 constant_dynamic-update-slice_fusion
  54.8 6.7 %collective-permute-start.13 = (bf16[16,144,128]{2,1,0:T(8,128)(2,1)S(1)}, bf16[16,144,128]{2,1,0:T(8,128)(2,1)S(1)}, u32[]{:S(2)}, u32[]{:S(2)}) collective-permute-start(bf16[16,144,128]{2,1,0:T(8,128)(2,1)S(1)} %get-tuple-element.67), channel_id=1, source_target_pairs={{0,4},{4,0},{8,12},{12,8},{16,20},{20,16},{24,28},{28,24},{32,36},... | collective-permute-start | bytes 1769480 | tf_op jit(solution)/shard_map/ppermute | solution.py:78
  61.5 2.8 %second_products.1 = (f32[512,1024]{1,0:T(8,128)S(1)}, f32[512,1024]{1,0:T(8,128)S(1)}, f32[512,1024]{1,0:T(8,128)S(1)}, f32[512,1024]{1,0:T(8,128)S(1)}) custom-call(bf16[1536,1024]{1,0:T(8,128)(2,1)S(1)} %bitcast.15, bf16[384,1024]{1,0:T(8,128)(2,1)S(1)} %collective-permute-done.11.right, ...), custom_call_target="tpu_custom_call", output_to_operand_aliasing={{0}: (3, {}), {1}: (4, {}), {2}: (5, {}), {3}: (6, {})} | custom-call | flops 1 | bytes 1 | tf_op jit(solution)/shard_map/second_products/pallas_call | solution.py:390
  64.3 0.0 collective-permute-done.13
  64.4 0.1 constant_dynamic-update-slice_fusion.5.got
  64.4 8.8 %newest.1 = (bf16[2048,1024]{1,0:T(8,128)(2,1)}, bf16[64,64,128]{2,1,0:T(8,128)(2,1)}) custom-call(s32[256]{0:T(256)S(1)} %select_reduce_fusion.1.head, s32[640]{0:T(1024)S(1)} %select_reduce_fusion.nxt.old_nxt, f32[16]{0:T(128)S(1)} %get-tuple-element.78.w1, f32[16]{0:T(128)S(1)} %get-tuple-element.77.w2, ...), custom_call_target="tpu_custom_call", output_to_operand_aliasing={{0}: (6, {})} | custom-call | flops 1 | bytes 1 | tf_op jit(solution)/shard_map/newest/pallas_call | solution.py:329
  73.3 0.0 collective-permute-done.14.low
  73.3 0.0 collective-permute-done.15.high
  73.3 3.8 %end.1 = bf16[2048,1024]{1,0:T(8,128)(2,1)} custom-call(s32[2]{0:T(128)S(1)} %bitcast.26, bf16[1536,1024]{1,0:T(8,128)(2,1)S(1)} %bitcast.16, bf16[384,1024]{1,0:T(8,128)(2,1)S(1)} %collective-permute-done.14.low, bf16[384,1024]{1,0:T(8,128)(2,1)S(1)} %collective-permute-done.15.high, f32[512,1024]{1,0:T(8,128)S(1)} %get-tuple-element.55.q0, ...), custom_call_target="tpu_custom_call" | custom-call | flops 1 | bytes 1 | tf_op jit(solution)/shard_map/end/pallas_call | solution.py:434
  (10 shorter events, 0.1 us)
Async XLA Ops:
  0.6 6.9 %collective-permute-start = (s32[2]{0:T(128)}, s32[2]{0:T(128)S(1)}, u32[]{:S(2)}, u32[]{:S(2)}) collective-permute-start(s32[2]{0:T(128)} %bitcast.23), channel_id=1, source_target_pairs={{0,1},{1,0},{2,3},{3,2},{4,5},{5,4},{6,7},{7,6},{8,9},{9,8},{10,11... | collective-permute-start | bytes 32 | tf_op jit(solution)/shard_map/ppermute | solution.py:61
  7.4 0.7 copy-start.2
  7.4 13.2 %copy-start = (bf16[1,1536,1024]{2,1,0:T(8,128)(2,1)S(1)}, bf16[1,1536,1024]{2,1,0:T(8,128)(2,1)}, u32[]{:S(2)}) copy-start(bf16[1,1536,1024]{2,1,0:T(8,128)(2,1)} %param.8) | copy-start | bytes 9437188
  8.1 3.6 %collective-permute-start.1 = (s32[4]{0:T(128)S(1)}, s32[4]{0:T(128)S(1)}, u32[]{:S(2)}, u32[]{:S(2)}) collective-permute-start(s32[4]{0:T(128)S(1)} %pad_add_fusion.near), channel_id=1, source_target_pairs={{0,3},{1,2},{2,1},{3,0},{4,7},{5,6},{6,5},{7,4},{8,11},{9,10},{10,... | collective-permute-start | bytes 56 | tf_op jit(solution)/shard_map/ppermute | solution.py:61
  12.7 6.5 %collective-permute-start.2 = (bf16[384,128]{1,0:T(8,128)(2,1)S(1)}, bf16[384,128]{1,0:T(8,128)(2,1)S(1)}, u32[]{:S(2)}, u32[]{:S(2)}) collective-permute-start(bf16[384,128]{1,0:T(8,128)(2,1)S(1)} %get-tuple-element.35), channel_id=1, source_target_pairs={{0,1},{1,0},{2,3},{3,2},{4,5},{5,4},{6,7},{7,6},{8,9},{9,8},{10,11... | collective-permute-start | bytes 294920 | tf_op jit(solution)/shard_map/ppermute | solution.py:61
  13.1 6.1 %collective-permute-start.3 = (bf16[384,128]{1,0:T(8,128)(2,1)S(1)}, bf16[384,128]{1,0:T(8,128)(2,1)S(1)}, u32[]{:S(2)}, u32[]{:S(2)}) collective-permute-start(bf16[384,128]{1,0:T(8,128)(2,1)S(1)} %get-tuple-element.36), channel_id=1, source_target_pairs={{0,3},{1,2},{2,1},{3,0},{4,7},{5,6},{6,5},{7,4},{8,11},{9,10},{10,... | collective-permute-start | bytes 294920 | tf_op jit(solution)/shard_map/ppermute | solution.py:61
  15.1 5.4 %collective-permute-start.4 = (bf16[384,128]{1,0:T(8,128)(2,1)S(1)}, bf16[384,128]{1,0:T(8,128)(2,1)S(1)}, u32[]{:S(2)}, u32[]{:S(2)}) collective-permute-start(bf16[384,128]{1,0:T(8,128)(2,1)S(1)} %get-tuple-element.37), channel_id=1, source_target_pairs={{0,2},{1,3},{2,0},{3,1},{4,6},{5,7},{6,4},{7,5},{8,10},{9,11},{10,... | collective-permute-start | bytes 294920 | tf_op jit(solution)/shard_map/ppermute | solution.py:61
  16.2 22.9 %collective-permute-start.8 = (bf16[384,1024]{1,0:T(8,128)(2,1)S(1)}, bf16[384,1024]{1,0:T(8,128)(2,1)S(1)}, u32[]{:S(2)}, u32[]{:S(2)}) collective-permute-start(bf16[384,1024]{1,0:T(8,128)(2,1)S(1)} %get-tuple-element.52), channel_id=1, source_target_pairs={{0,1},{1,2},{2,3},{3,0},{4,5},{5,6},{6,7},{7,4},{8,9},{9,10},{10,1... | collective-permute-start | bytes 2359304 | tf_op jit(solution)/shard_map/ppermute | solution.py:54
  16.3 22.8 %collective-permute-start.9 = (bf16[384,1024]{1,0:T(8,128)(2,1)S(1)}, bf16[384,1024]{1,0:T(8,128)(2,1)S(1)}, u32[]{:S(2)}, u32[]{:S(2)}) collective-permute-start(bf16[384,1024]{1,0:T(8,128)(2,1)S(1)} %get-tuple-element.51), channel_id=1, source_target_pairs={{0,3},{1,0},{2,1},{3,2},{4,7},{5,4},{6,5},{7,6},{8,11},{9,8},{10,9... | collective-permute-start | bytes 2359304 | tf_op jit(solution)/shard_map/ppermute | solution.py:54
  22.3 4.9 %collective-permute-start.5 = (bf16[1,144,128]{2,1,0:T(8,128)(2,1)S(1)}, bf16[1,144,128]{2,1,0:T(8,128)(2,1)S(1)}, u32[]{:S(2)}, u32[]{:S(2)}) collective-permute-start(bf16[1,144,128]{2,1,0:T(8,128)(2,1)S(1)} %bitcast.19), channel_id=1, source_target_pairs={{0,8},{4,12},{8,0},{12,4},{16,24},{20,28},{24,16},{28,20},{32,40},... | collective-permute-start | bytes 110600 | tf_op jit(solution)/shard_map/ppermute | solution.py:78
  27.3 10.5 %collective-permute-start.6 = (bf16[2,144,128]{2,1,0:T(8,128)(2,1)S(1)}, bf16[2,144,128]{2,1,0:T(8,128)(2,1)S(1)}, u32[]{:S(2)}, u32[]{:S(2)}) collective-permute-start(bf16[2,144,128]{2,1,0:T(8,128)(2,1)S(1)} %pad_maximum_fusion.2), channel_id=1, source_target_pairs={{0,24},{4,28},{8,16},{12,20},{16,8},{20,12},{24,0},{28,4},{32,56},... | collective-permute-start | bytes 221192 | tf_op jit(solution)/shard_map/ppermute | solution.py:78
  29.3 25.4 %collective-permute-start.11 = (bf16[384,1024]{1,0:T(8,128)(2,1)S(1)}, bf16[384,1024]{1,0:T(8,128)(2,1)S(1)}, u32[]{:S(2)}, u32[]{:S(2)}) collective-permute-start(bf16[384,1024]{1,0:T(8,128)(2,1)S(1)} %get-tuple-element.51), channel_id=1, source_target_pairs={{0,1},{1,2},{2,3},{3,0},{4,5},{5,6},{6,7},{7,4},{8,9},{9,10},{10,1... | collective-permute-start | bytes 2359304 | tf_op jit(solution)/shard_map/ppermute | solution.py:54
  30.1 24.5 %collective-permute-start.12 = (bf16[384,1024]{1,0:T(8,128)(2,1)S(1)}, bf16[384,1024]{1,0:T(8,128)(2,1)S(1)}, u32[]{:S(2)}, u32[]{:S(2)}) collective-permute-start(bf16[384,1024]{1,0:T(8,128)(2,1)S(1)} %get-tuple-element.52), channel_id=1, source_target_pairs={{0,3},{1,0},{2,1},{3,2},{4,7},{5,4},{6,5},{7,6},{8,11},{9,8},{10,9... | collective-permute-start | bytes 2359304 | tf_op jit(solution)/shard_map/ppermute | solution.py:54
  32.0 7.1 %copy-start.1 = (bf16[1,2048,1024]{2,1,0:T(8,128)(2,1)S(1)}, bf16[1,2048,1024]{2,1,0:T(8,128)(2,1)}, u32[]{:S(2)}) copy-start(bf16[1,2048,1024]{2,1,0:T(8,128)(2,1)} %param.9) | copy-start | bytes 12582916
  37.8 5.9 %collective-permute-start.7 = (bf16[4,144,128]{2,1,0:T(8,128)(2,1)S(1)}, bf16[4,144,128]{2,1,0:T(8,128)(2,1)S(1)}, u32[]{:S(2)}, u32[]{:S(2)}) collective-permute-start(bf16[4,144,128]{2,1,0:T(8,128)(2,1)S(1)} %pad_maximum_fusion.1), channel_id=1, source_target_pairs={{0,32},{4,36},{8,40},{12,44},{16,48},{20,52},{24,56},{28,60},{32,0... | collective-permute-start | bytes 442376 | tf_op jit(solution)/shard_map/ppermute | solution.py:78
  43.7 10.9 %collective-permute-start.10 = (bf16[8,144,128]{2,1,0:T(8,128)(2,1)S(1)}, bf16[8,144,128]{2,1,0:T(8,128)(2,1)S(1)}, u32[]{:S(2)}, u32[]{:S(2)}) collective-permute-start(bf16[8,144,128]{2,1,0:T(8,128)(2,1)S(1)} %pad_maximum_fusion), channel_id=1, source_target_pairs={{0,96},{4,100},{8,104},{12,108},{16,112},{20,116},{24,120},{28,124... | collective-permute-start | bytes 884744 | tf_op jit(solution)/shard_map/ppermute | solution.py:78
  45.7 27.6 %collective-permute-start.14 = (bf16[384,1024]{1,0:T(8,128)(2,1)S(1)}, bf16[384,1024]{1,0:T(8,128)(2,1)S(1)}, u32[]{:S(2)}, u32[]{:S(2)}) collective-permute-start(bf16[384,1024]{1,0:T(8,128)(2,1)S(1)} %collective-permute-done.8.right), channel_id=1, source_target_pairs={{0,1},{1,2},{2,3},{3,0},{4,5},{5,6},{6,7},{7,4},{8,9},{9,10},{10,1... | collective-permute-start | bytes 2359304 | tf_op jit(solution)/shard_map/ppermute | solution.py:54
  45.8 27.5 %collective-permute-start.15 = (bf16[384,1024]{1,0:T(8,128)(2,1)S(1)}, bf16[384,1024]{1,0:T(8,128)(2,1)S(1)}, u32[]{:S(2)}, u32[]{:S(2)}) collective-permute-start(bf16[384,1024]{1,0:T(8,128)(2,1)S(1)} %collective-permute-done.9.left), channel_id=1, source_target_pairs={{0,3},{1,0},{2,1},{3,2},{4,7},{5,4},{6,5},{7,6},{8,11},{9,8},{10,9... | collective-permute-start | bytes 2359304 | tf_op jit(solution)/shard_map/ppermute | solution.py:54
  54.8 9.6 %collective-permute-start.13 = (bf16[16,144,128]{2,1,0:T(8,128)(2,1)S(1)}, bf16[16,144,128]{2,1,0:T(8,128)(2,1)S(1)}, u32[]{:S(2)}, u32[]{:S(2)}) collective-permute-start(bf16[16,144,128]{2,1,0:T(8,128)(2,1)S(1)} %get-tuple-element.67), channel_id=1, source_target_pairs={{0,4},{4,0},{8,12},{12,8},{16,20},{20,16},{24,28},{28,24},{32,36},... | collective-permute-start | bytes 1769480 | tf_op jit(solution)/shard_map/ppermute | solution.py:78

commit v4 on v3

--- a/solution.py
+++ b/solution.py
@@ -399,7 +399,7 @@
     )(up, right, left, *totals)
 
 
-NSPLIT = 2
+NSPLIT = 1
 
 
 def end_kernel(chosen, up, low, high, q0, q1, q2, q3, out, staged, sem):

time: 77.6 us -> 77.5 us (level)
  no operation moved by 1% of the time
where the time goes in v4:
time: 77.5 us; the launch traced here: 77.1 us
  Pallas kernels  39 us (50%)
  starting transfers between devices  29.7 us (38%)
  waiting for transfers between devices  3 us (4%)
  other arithmetic  1.99 us (3%)
  between operations  1.7 us (2%)
  local copies, waits for them, and re-layouts  1.66 us (2%)
    ppermute x5, starting transfers between devices, dp_exchange(): received = lax.ppermute(value, 'dp', pairs)  13.3 us
    pallas_call x2, Pallas kernels, window(): pl.pallas_call(functools.partial(window_kernel, base), out_shape=jax.Shap...  11.7 us
    pallas_call x1, Pallas kernels, newest(): pl.pallas_call(newest_kernel, out_shape=(jax.ShapeDtypeStruct((D, QS), BF...  8.47 us
    ppermute x5, starting transfers between devices, pass_on(): return lax.ppermute(x, 'tensor', [(i, i ^ flip) for i in range(NZ)])  8.3 us
    ppermute x6, starting transfers between devices, shift(): return lax.ppermute(x, axis, [(i, (i + step) % size) for i in range(size)])  8.16 us
    pallas_call x2, Pallas kernels, load(): pl.pallas_call(load_kernel, out_shape=jax.ShapeDtypeStruct(source.shape,...  4.81 us
    pallas_call x1, Pallas kernels, first_products(): pl.pallas_call(first_kernel, out_shape=[ACC] * 4, in_specs=[whole(VMEM)]...  4.57 us
    pallas_call x1, Pallas kernels, end(): pl.pallas_call(end_kernel, out_shape=jax.ShapeDtypeStruct((D, QS), BF16),...  3.98 us
  transfers between devices with their start and end apart: 16, of which 3 were waited for; matrix products, arithmetic and copies ran while one was open for 4% of the time, Pallas kernels for 44%

profile of v4, /device:TPU:1, one launch (start us, length us, event | category | flops | bytes accessed | tf_op | source)
XLA Modules:
  0.0 77.1 jit_solution(8032111095850276426)
XLA Ops:
  0.6 2.5 %collective-permute-start = (s32[2]{0:T(128)}, s32[2]{0:T(128)S(1)}, u32[]{:S(2)}, u32[]{:S(2)}) collective-permute-start(s32[2]{0:T(128)} %bitcast.23), channel_id=1, source_target_pairs={{0,1},{1,0},{2,3},{3,2},{4,5},{5,4},{6,7},{7,6},{8,9},{9,8},{10,11... | collective-permute-start | bytes 32 | tf_op jit(solution)/shard_map/ppermute | solution.py:61
  3.8 0.1 broadcast_in_dim.58
  3.9 0.1 broadcast_in_dim.59
  4.0 0.5 broadcast.62
  4.5 1.3 %reduce.3 = s32[8,64]{1,0:T(8,128)S(1)} reduce(s32[8,1,64]{2,1,0:T(1,128)} %param.12, s32[]{:T(128)} %broadcast.62), dimensions={1}, to_apply=%param.12.reduce_sub_computation.3 | reduce | bytes 4100 | tf_op args[5]
  5.9 0.1 reshape.32
  5.9 1.4 %load.2.tokens = bf16[384,2048]{1,0:T(8,128)(2,1)S(1)} custom-call(bf16[384,2048]{1,0:T(8,128)(2,1)} %bitcast.29), custom_call_target="tpu_custom_call" | custom-call | flops 1 | bytes 1 | tf_op jit(solution)/shard_map/load/pallas_call | solution.py:95
  7.4 0.0 copy-start.2
  7.4 0.0 copy-start
  7.4 0.1 fusion.3
  7.6 0.0 collective-permute-done
  7.6 0.5 copy-done.2
  8.0 0.1 pad_add_fusion.near
  8.1 2.2 %collective-permute-start.1 = (s32[4]{0:T(128)S(1)}, s32[4]{0:T(128)S(1)}, u32[]{:S(2)}, u32[]{:S(2)}) collective-permute-start(s32[4]{0:T(128)S(1)} %pad_add_fusion.near), channel_id=1, source_target_pairs={{0,3},{1,2},{2,1},{3,0},{4,7},{5,6},{6,5},{7,4},{8,11},{9,10},{10,... | collective-permute-start | bytes 56 | tf_op jit(solution)/shard_map/ppermute | solution.py:61
  10.3 1.4 %collective-permute-done.1.across = s32[4]{0:T(128)S(1)} collective-permute-done((s32[4]{0:T(128)S(1)}, s32[4]{0:T(128)S(1)}, u32[]{:S(2)}, u32[]{:S(2)}) %collective-permute-start.1) | collective-permute-done | bytes 48 | tf_op jit(solution)/shard_map/ppermute | solution.py:61
  11.7 1.0 %reply.1 = (bf16[384,128]{1,0:T(8,128)(2,1)S(1)}, bf16[384,128]{1,0:T(8,128)(2,1)S(1)}, bf16[384,128]{1,0:T(8,128)(2,1)S(1)}, bf16[384,128]{1,0:T(8,128)(2,1)S(1)}) custom-call(s32[4]{0:T(128)S(1)} %pad_add_fusion.near, s32[4]{0:T(128)S(1)} %collective-permute-done.1.across, bf16[384,2048]{1,0:T(8,128)(2,1)S(1)} %load.2.tokens), custom_call_target="tpu_custom_call" | custom-call | flops 1 | bytes 1 | tf_op jit(solution)/shard_map/reply/pallas_call | solution.py:122
  12.7 0.4 collective-permute-start.2
  13.1 2.1 %collective-permute-start.3 = (bf16[384,128]{1,0:T(8,128)(2,1)S(1)}, bf16[384,128]{1,0:T(8,128)(2,1)S(1)}, u32[]{:S(2)}, u32[]{:S(2)}) collective-permute-start(bf16[384,128]{1,0:T(8,128)(2,1)S(1)} %get-tuple-element.36), channel_id=1, source_target_pairs={{0,3},{1,2},{2,1},{3,0},{4,7},{5,6},{6,5},{7,4},{8,11},{9,10},{10,... | collective-permute-start | bytes 294920 | tf_op jit(solution)/shard_map/ppermute | solution.py:61
  15.1 1.0 %collective-permute-start.4 = (bf16[384,128]{1,0:T(8,128)(2,1)S(1)}, bf16[384,128]{1,0:T(8,128)(2,1)S(1)}, u32[]{:S(2)}, u32[]{:S(2)}) collective-permute-start(bf16[384,128]{1,0:T(8,128)(2,1)S(1)} %get-tuple-element.37), channel_id=1, source_target_pairs={{0,2},{1,3},{2,0},{3,1},{4,6},{5,7},{6,4},{7,5},{8,10},{9,11},{10,... | collective-permute-start | bytes 294920 | tf_op jit(solution)/shard_map/ppermute | solution.py:61
  16.2 0.1 collective-permute-start.8
  16.3 2.5 %collective-permute-start.9 = (bf16[384,1024]{1,0:T(8,128)(2,1)S(1)}, bf16[384,1024]{1,0:T(8,128)(2,1)S(1)}, u32[]{:S(2)}, u32[]{:S(2)}) collective-permute-start(bf16[384,1024]{1,0:T(8,128)(2,1)S(1)} %get-tuple-element.51), channel_id=1, source_target_pairs={{0,3},{1,0},{2,1},{3,2},{4,7},{5,4},{6,5},{7,6},{8,11},{9,8},{10,9... | collective-permute-start | bytes 2359304 | tf_op jit(solution)/shard_map/ppermute | solution.py:54
  18.9 0.3 select_reduce_fusion.nxt.old_nxt
  19.2 0.0 collective-permute-done.2.c1
  19.2 0.0 collective-permute-done.3.c2
  19.2 1.3 %collective-permute-done.4.c3 = bf16[384,128]{1,0:T(8,128)(2,1)S(1)} collective-permute-done((bf16[384,128]{1,0:T(8,128)(2,1)S(1)}, bf16[384,128]{1,0:T(8,128)(2,1)S(1)}, u32[]{:S(2)}, u32[]{:S(2)}) %collective-permute-start.4) | collective-permute-done | bytes 98336 | tf_op jit(solution)/shard_map/ppermute | solution.py:61
  20.6 0.0 copy-done
  20.6 1.7 %pick.1 = bf16[144,128]{1,0:T(8,128)(2,1)S(1)} custom-call(s32[2]{0:T(128)S(1)} %bitcast.25, bf16[1536,1024]{1,0:T(8,128)(2,1)S(1)} %bitcast.13, bf16[2048,1024]{1,0:T(8,128)(2,1)} %bitcast.17, bf16[384,128]{1,0:T(8,128)(2,1)S(1)} %get-tuple-element.34.own, bf16[384,128]{1,0:T(8,128)(2,1)S(1)} %collective-permute-done.2.c1, ...), custom_call_target="tpu_custom_call" | custom-call | flops 1 | bytes 1 | tf_op jit(solution)/shard_map/pick/pallas_call | solution.py:163
  22.3 1.4 %collective-permute-start.5 = (bf16[1,144,128]{2,1,0:T(8,128)(2,1)S(1)}, bf16[1,144,128]{2,1,0:T(8,128)(2,1)S(1)}, u32[]{:S(2)}, u32[]{:S(2)}) collective-permute-start(bf16[1,144,128]{2,1,0:T(8,128)(2,1)S(1)} %bitcast.19), channel_id=1, source_target_pairs={{0,8},{4,12},{8,0},{12,4},{16,24},{20,28},{24,16},{28,20},{32,40},... | collective-permute-start | bytes 110600 | tf_op jit(solution)/shard_map/ppermute | solution.py:78
  23.7 0.1 select_reduce_fusion.1.head
  23.9 3.4 %load.3.vals = bf16[512,64,128]{2,1,0:T(8,128)(2,1)S(1)} custom-call(bf16[512,64,128]{2,1,0:T(8,128)(2,1)} %bitcast.27), custom_call_target="tpu_custom_call" | custom-call | flops 1 | bytes 1 | tf_op jit(solution)/shard_map/load/pallas_call | solution.py:95
  27.3 0.0 collective-permute-done.5
  27.3 2.0 %collective-permute-start.6 = (bf16[2,144,128]{2,1,0:T(8,128)(2,1)S(1)}, bf16[2,144,128]{2,1,0:T(8,128)(2,1)S(1)}, u32[]{:S(2)}, u32[]{:S(2)}) collective-permute-start(bf16[2,144,128]{2,1,0:T(8,128)(2,1)S(1)} %pad_maximum_fusion.2), channel_id=1, source_target_pairs={{0,24},{4,28},{8,16},{12,20},{16,8},{20,12},{24,0},{28,4},{32,56},... | collective-permute-start | bytes 221192 | tf_op jit(solution)/shard_map/ppermute | solution.py:78
  29.3 0.9 %collective-permute-start.11 = (bf16[384,1024]{1,0:T(8,128)(2,1)S(1)}, bf16[384,1024]{1,0:T(8,128)(2,1)S(1)}, u32[]{:S(2)}, u32[]{:S(2)}) collective-permute-start(bf16[384,1024]{1,0:T(8,128)(2,1)S(1)} %get-tuple-element.51), channel_id=1, source_target_pairs={{0,1},{1,2},{2,3},{3,0},{4,5},{5,6},{6,7},{7,4},{8,9},{9,10},{10,1... | collective-permute-start | bytes 2359304 | tf_op jit(solution)/shard_map/ppermute | solution.py:54
  30.2 1.8 %collective-permute-start.12 = (bf16[384,1024]{1,0:T(8,128)(2,1)S(1)}, bf16[384,1024]{1,0:T(8,128)(2,1)S(1)}, u32[]{:S(2)}, u32[]{:S(2)}) collective-permute-start(bf16[384,1024]{1,0:T(8,128)(2,1)S(1)} %get-tuple-element.52), channel_id=1, source_target_pairs={{0,3},{1,0},{2,1},{3,2},{4,7},{5,4},{6,5},{7,6},{8,11},{9,8},{10,9... | collective-permute-start | bytes 2359304 | tf_op jit(solution)/shard_map/ppermute | solution.py:54
  32.0 0.0 copy-start.1
  32.0 5.9 %window.2.refs_0_ = bf16[2048,1024]{1,0:T(8,128)(2,1)} custom-call(s32[256]{0:T(256)S(1)} %select_reduce_fusion.1.head, s32[640]{0:T(1024)S(1)} %select_reduce_fusion.nxt.old_nxt, f32[16]{0:T(128)S(1)} %get-tuple-element.78.w1, f32[16]{0:T(128)S(1)} %get-tuple-element.77.w2, bf16[512,64,128]{2,1,0:T(8,128)(2,1)S(1)} %load.3.vals), custom_call_target="tpu_custom_call" | custom-call | flops 1 | bytes 1 | tf_op jit(solution)/shard_map/window/pallas_call | solution.py:224
  37.9 0.0 collective-permute-done.6
  38.0 1.3 %collective-permute-start.7 = (bf16[4,144,128]{2,1,0:T(8,128)(2,1)S(1)}, bf16[4,144,128]{2,1,0:T(8,128)(2,1)S(1)}, u32[]{:S(2)}, u32[]{:S(2)}) collective-permute-start(bf16[4,144,128]{2,1,0:T(8,128)(2,1)S(1)} %pad_maximum_fusion.1), channel_id=1, source_target_pairs={{0,32},{4,36},{8,40},{12,44},{16,48},{20,52},{24,56},{28,60},{32,0... | collective-permute-start | bytes 442376 | tf_op jit(solution)/shard_map/ppermute | solution.py:78
  39.3 0.0 collective-permute-done.8.right
  39.3 0.0 collective-permute-done.9.left
  39.3 0.0 copy-done.1
  39.3 4.6 %first_products.1 = (f32[512,1024]{1,0:T(8,128)S(1)}, f32[512,1024]{1,0:T(8,128)S(1)}, f32[512,1024]{1,0:T(8,128)S(1)}, f32[512,1024]{1,0:T(8,128)S(1)}) custom-call(bf16[1536,1024]{1,0:T(8,128)(2,1)S(1)} %bitcast.14, bf16[2048,1024]{1,0:T(8,128)(2,1)S(1)} %bitcast.18, bf16[384,2048]{1,0:T(8,128)(2,1)S(1)} %load.2.tokens, ...), custom_call_target="tpu_custom_call" | custom-call | flops 1 | bytes 1 | tf_op jit(solution)/shard_map/first_products/pallas_call | solution.py:371
  43.9 0.0 collective-permute-done.7
  43.9 1.9 %collective-permute-start.10 = (bf16[8,144,128]{2,1,0:T(8,128)(2,1)S(1)}, bf16[8,144,128]{2,1,0:T(8,128)(2,1)S(1)}, u32[]{:S(2)}, u32[]{:S(2)}) collective-permute-start(bf16[8,144,128]{2,1,0:T(8,128)(2,1)S(1)} %pad_maximum_fusion), channel_id=1, source_target_pairs={{0,96},{4,100},{8,104},{12,108},{16,112},{20,116},{24,120},{28,124... | collective-permute-start | bytes 884744 | tf_op jit(solution)/shard_map/ppermute | solution.py:78
  45.9 0.1 collective-permute-start.14
  45.9 2.7 %collective-permute-start.15 = (bf16[384,1024]{1,0:T(8,128)(2,1)S(1)}, bf16[384,1024]{1,0:T(8,128)(2,1)S(1)}, u32[]{:S(2)}, u32[]{:S(2)}) collective-permute-start(bf16[384,1024]{1,0:T(8,128)(2,1)S(1)} %collective-permute-done.9.left), channel_id=1, source_target_pairs={{0,3},{1,0},{2,1},{3,2},{4,7},{5,4},{6,5},{7,6},{8,11},{9,8},{10,9... | collective-permute-start | bytes 2359304 | tf_op jit(solution)/shard_map/ppermute | solution.py:54
  48.6 5.7 %window.3.update = bf16[2048,1024]{1,0:T(8,128)(2,1)} custom-call(s32[256]{0:T(256)S(1)} %select_reduce_fusion.1.head, s32[640]{0:T(1024)S(1)} %select_reduce_fusion.nxt.old_nxt, f32[16]{0:T(128)S(1)} %get-tuple-element.78.w1, f32[16]{0:T(128)S(1)} %get-tuple-element.77.w2, bf16[512,64,128]{2,1,0:T(8,128)(2,1)S(1)} %load.3.vals, ...), custom_call_target="tpu_custom_call", output_to_operand_aliasing={{}: (5, {})} | custom-call | flops 1 | bytes 1 | tf_op jit(solution)/shard_map/window/pallas_call | solution.py:224
  54.3 0.1 constant_dynamic-update-slice_fusion.1
  54.4 0.3 collective-permute-done.11.right
  54.7 0.0 collective-permute-done.12.left
  54.7 0.0 collective-permute-done.10
  54.7 0.1 constant_dynamic-update-slice_fusion
  54.8 6.7 %collective-permute-start.13 = (bf16[16,144,128]{2,1,0:T(8,128)(2,1)S(1)}, bf16[16,144,128]{2,1,0:T(8,128)(2,1)S(1)}, u32[]{:S(2)}, u32[]{:S(2)}) collective-permute-start(bf16[16,144,128]{2,1,0:T(8,128)(2,1)S(1)} %get-tuple-element.67), channel_id=1, source_target_pairs={{0,4},{4,0},{8,12},{12,8},{16,20},{20,16},{24,28},{28,24},{32,36},... | collective-permute-start | bytes 1769480 | tf_op jit(solution)/shard_map/ppermute | solution.py:78
  61.5 2.8 %second_products.1 = (f32[512,1024]{1,0:T(8,128)S(1)}, f32[512,1024]{1,0:T(8,128)S(1)}, f32[512,1024]{1,0:T(8,128)S(1)}, f32[512,1024]{1,0:T(8,128)S(1)}) custom-call(bf16[1536,1024]{1,0:T(8,128)(2,1)S(1)} %bitcast.15, bf16[384,1024]{1,0:T(8,128)(2,1)S(1)} %collective-permute-done.11.right, ...), custom_call_target="tpu_custom_call", output_to_operand_aliasing={{0}: (3, {}), {1}: (4, {}), {2}: (5, {}), {3}: (6, {})} | custom-call | flops 1 | bytes 1 | tf_op jit(solution)/shard_map/second_products/pallas_call | solution.py:390
  64.4 0.0 collective-permute-done.13
  64.4 0.1 constant_dynamic-update-slice_fusion.5.got
  64.5 8.5 %newest.1 = (bf16[2048,1024]{1,0:T(8,128)(2,1)}, bf16[64,64,128]{2,1,0:T(8,128)(2,1)}) custom-call(s32[256]{0:T(256)S(1)} %select_reduce_fusion.1.head, s32[640]{0:T(1024)S(1)} %select_reduce_fusion.nxt.old_nxt, f32[16]{0:T(128)S(1)} %get-tuple-element.78.w1, f32[16]{0:T(128)S(1)} %get-tuple-element.77.w2, ...), custom_call_target="tpu_custom_call", output_to_operand_aliasing={{0}: (6, {})} | custom-call | flops 1 | bytes 1 | tf_op jit(solution)/shard_map/newest/pallas_call | solution.py:329
  72.9 0.0 collective-permute-done.14.low
  72.9 0.0 collective-permute-done.15.high
  73.0 4.0 %end.1 = bf16[2048,1024]{1,0:T(8,128)(2,1)} custom-call(s32[2]{0:T(128)S(1)} %bitcast.26, bf16[1536,1024]{1,0:T(8,128)(2,1)S(1)} %bitcast.16, bf16[384,1024]{1,0:T(8,128)(2,1)S(1)} %collective-permute-done.14.low, bf16[384,1024]{1,0:T(8,128)(2,1)S(1)} %collective-permute-done.15.high, f32[512,1024]{1,0:T(8,128)S(1)} %get-tuple-element.55.q0, ...), custom_call_target="tpu_custom_call" | custom-call | flops 1 | bytes 1 | tf_op jit(solution)/shard_map/end/pallas_call | solution.py:434
  (10 shorter events, 0.1 us)
Async XLA Ops:
  0.6 6.9 %collective-permute-start = (s32[2]{0:T(128)}, s32[2]{0:T(128)S(1)}, u32[]{:S(2)}, u32[]{:S(2)}) collective-permute-start(s32[2]{0:T(128)} %bitcast.23), channel_id=1, source_target_pairs={{0,1},{1,0},{2,3},{3,2},{4,5},{5,4},{6,7},{7,6},{8,9},{9,8},{10,11... | collective-permute-start | bytes 32 | tf_op jit(solution)/shard_map/ppermute | solution.py:61
  7.4 0.7 copy-start.2
  7.4 13.2 %copy-start = (bf16[1,1536,1024]{2,1,0:T(8,128)(2,1)S(1)}, bf16[1,1536,1024]{2,1,0:T(8,128)(2,1)}, u32[]{:S(2)}) copy-start(bf16[1,1536,1024]{2,1,0:T(8,128)(2,1)} %param.8) | copy-start | bytes 9437188
  8.1 3.6 %collective-permute-start.1 = (s32[4]{0:T(128)S(1)}, s32[4]{0:T(128)S(1)}, u32[]{:S(2)}, u32[]{:S(2)}) collective-permute-start(s32[4]{0:T(128)S(1)} %pad_add_fusion.near), channel_id=1, source_target_pairs={{0,3},{1,2},{2,1},{3,0},{4,7},{5,6},{6,5},{7,4},{8,11},{9,10},{10,... | collective-permute-start | bytes 56 | tf_op jit(solution)/shard_map/ppermute | solution.py:61
  12.7 6.5 %collective-permute-start.2 = (bf16[384,128]{1,0:T(8,128)(2,1)S(1)}, bf16[384,128]{1,0:T(8,128)(2,1)S(1)}, u32[]{:S(2)}, u32[]{:S(2)}) collective-permute-start(bf16[384,128]{1,0:T(8,128)(2,1)S(1)} %get-tuple-element.35), channel_id=1, source_target_pairs={{0,1},{1,0},{2,3},{3,2},{4,5},{5,4},{6,7},{7,6},{8,9},{9,8},{10,11... | collective-permute-start | bytes 294920 | tf_op jit(solution)/shard_map/ppermute | solution.py:61
  13.1 6.1 %collective-permute-start.3 = (bf16[384,128]{1,0:T(8,128)(2,1)S(1)}, bf16[384,128]{1,0:T(8,128)(2,1)S(1)}, u32[]{:S(2)}, u32[]{:S(2)}) collective-permute-start(bf16[384,128]{1,0:T(8,128)(2,1)S(1)} %get-tuple-element.36), channel_id=1, source_target_pairs={{0,3},{1,2},{2,1},{3,0},{4,7},{5,6},{6,5},{7,4},{8,11},{9,10},{10,... | collective-permute-start | bytes 294920 | tf_op jit(solution)/shard_map/ppermute | solution.py:61
  15.1 5.4 %collective-permute-start.4 = (bf16[384,128]{1,0:T(8,128)(2,1)S(1)}, bf16[384,128]{1,0:T(8,128)(2,1)S(1)}, u32[]{:S(2)}, u32[]{:S(2)}) collective-permute-start(bf16[384,128]{1,0:T(8,128)(2,1)S(1)} %get-tuple-element.37), channel_id=1, source_target_pairs={{0,2},{1,3},{2,0},{3,1},{4,6},{5,7},{6,4},{7,5},{8,10},{9,11},{10,... | collective-permute-start | bytes 294920 | tf_op jit(solution)/shard_map/ppermute | solution.py:61
  16.2 23.1 %collective-permute-start.8 = (bf16[384,1024]{1,0:T(8,128)(2,1)S(1)}, bf16[384,1024]{1,0:T(8,128)(2,1)S(1)}, u32[]{:S(2)}, u32[]{:S(2)}) collective-permute-start(bf16[384,1024]{1,0:T(8,128)(2,1)S(1)} %get-tuple-element.52), channel_id=1, source_target_pairs={{0,1},{1,2},{2,3},{3,0},{4,5},{5,6},{6,7},{7,4},{8,9},{9,10},{10,1... | collective-permute-start | bytes 2359304 | tf_op jit(solution)/shard_map/ppermute | solution.py:54
  16.3 22.9 %collective-permute-start.9 = (bf16[384,1024]{1,0:T(8,128)(2,1)S(1)}, bf16[384,1024]{1,0:T(8,128)(2,1)S(1)}, u32[]{:S(2)}, u32[]{:S(2)}) collective-permute-start(bf16[384,1024]{1,0:T(8,128)(2,1)S(1)} %get-tuple-element.51), channel_id=1, source_target_pairs={{0,3},{1,0},{2,1},{3,2},{4,7},{5,4},{6,5},{7,6},{8,11},{9,8},{10,9... | collective-permute-start | bytes 2359304 | tf_op jit(solution)/shard_map/ppermute | solution.py:54
  22.3 4.9 %collective-permute-start.5 = (bf16[1,144,128]{2,1,0:T(8,128)(2,1)S(1)}, bf16[1,144,128]{2,1,0:T(8,128)(2,1)S(1)}, u32[]{:S(2)}, u32[]{:S(2)}) collective-permute-start(bf16[1,144,128]{2,1,0:T(8,128)(2,1)S(1)} %bitcast.19), channel_id=1, source_target_pairs={{0,8},{4,12},{8,0},{12,4},{16,24},{20,28},{24,16},{28,20},{32,40},... | collective-permute-start | bytes 110600 | tf_op jit(solution)/shard_map/ppermute | solution.py:78
  27.3 10.7 %collective-permute-start.6 = (bf16[2,144,128]{2,1,0:T(8,128)(2,1)S(1)}, bf16[2,144,128]{2,1,0:T(8,128)(2,1)S(1)}, u32[]{:S(2)}, u32[]{:S(2)}) collective-permute-start(bf16[2,144,128]{2,1,0:T(8,128)(2,1)S(1)} %pad_maximum_fusion.2), channel_id=1, source_target_pairs={{0,24},{4,28},{8,16},{12,20},{16,8},{20,12},{24,0},{28,4},{32,56},... | collective-permute-start | bytes 221192 | tf_op jit(solution)/shard_map/ppermute | solution.py:78
  29.3 25.4 %collective-permute-start.11 = (bf16[384,1024]{1,0:T(8,128)(2,1)S(1)}, bf16[384,1024]{1,0:T(8,128)(2,1)S(1)}, u32[]{:S(2)}, u32[]{:S(2)}) collective-permute-start(bf16[384,1024]{1,0:T(8,128)(2,1)S(1)} %get-tuple-element.51), channel_id=1, source_target_pairs={{0,1},{1,2},{2,3},{3,0},{4,5},{5,6},{6,7},{7,4},{8,9},{9,10},{10,1... | collective-permute-start | bytes 2359304 | tf_op jit(solution)/shard_map/ppermute | solution.py:54
  30.2 24.5 %collective-permute-start.12 = (bf16[384,1024]{1,0:T(8,128)(2,1)S(1)}, bf16[384,1024]{1,0:T(8,128)(2,1)S(1)}, u32[]{:S(2)}, u32[]{:S(2)}) collective-permute-start(bf16[384,1024]{1,0:T(8,128)(2,1)S(1)} %get-tuple-element.52), channel_id=1, source_target_pairs={{0,3},{1,0},{2,1},{3,2},{4,7},{5,4},{6,5},{7,6},{8,11},{9,8},{10,9... | collective-permute-start | bytes 2359304 | tf_op jit(solution)/shard_map/ppermute | solution.py:54
  32.0 7.3 %copy-start.1 = (bf16[1,2048,1024]{2,1,0:T(8,128)(2,1)S(1)}, bf16[1,2048,1024]{2,1,0:T(8,128)(2,1)}, u32[]{:S(2)}) copy-start(bf16[1,2048,1024]{2,1,0:T(8,128)(2,1)} %param.9) | copy-start | bytes 12582916
  38.0 5.9 %collective-permute-start.7 = (bf16[4,144,128]{2,1,0:T(8,128)(2,1)S(1)}, bf16[4,144,128]{2,1,0:T(8,128)(2,1)S(1)}, u32[]{:S(2)}, u32[]{:S(2)}) collective-permute-start(bf16[4,144,128]{2,1,0:T(8,128)(2,1)S(1)} %pad_maximum_fusion.1), channel_id=1, source_target_pairs={{0,32},{4,36},{8,40},{12,44},{16,48},{20,52},{24,56},{28,60},{32,0... | collective-permute-start | bytes 442376 | tf_op jit(solution)/shard_map/ppermute | solution.py:78
  43.9 10.8 %collective-permute-start.10 = (bf16[8,144,128]{2,1,0:T(8,128)(2,1)S(1)}, bf16[8,144,128]{2,1,0:T(8,128)(2,1)S(1)}, u32[]{:S(2)}, u32[]{:S(2)}) collective-permute-start(bf16[8,144,128]{2,1,0:T(8,128)(2,1)S(1)} %pad_maximum_fusion), channel_id=1, source_target_pairs={{0,96},{4,100},{8,104},{12,108},{16,112},{20,116},{24,120},{28,124... | collective-permute-start | bytes 884744 | tf_op jit(solution)/shard_map/ppermute | solution.py:78
  45.9 27.1 %collective-permute-start.14 = (bf16[384,1024]{1,0:T(8,128)(2,1)S(1)}, bf16[384,1024]{1,0:T(8,128)(2,1)S(1)}, u32[]{:S(2)}, u32[]{:S(2)}) collective-permute-start(bf16[384,1024]{1,0:T(8,128)(2,1)S(1)} %collective-permute-done.8.right), channel_id=1, source_target_pairs={{0,1},{1,2},{2,3},{3,0},{4,5},{5,6},{6,7},{7,4},{8,9},{9,10},{10,1... | collective-permute-start | bytes 2359304 | tf_op jit(solution)/shard_map/ppermute | solution.py:54
  45.9 27.0 %collective-permute-start.15 = (bf16[384,1024]{1,0:T(8,128)(2,1)S(1)}, bf16[384,1024]{1,0:T(8,128)(2,1)S(1)}, u32[]{:S(2)}, u32[]{:S(2)}) collective-permute-start(bf16[384,1024]{1,0:T(8,128)(2,1)S(1)} %collective-permute-done.9.left), channel_id=1, source_target_pairs={{0,3},{1,0},{2,1},{3,2},{4,7},{5,4},{6,5},{7,6},{8,11},{9,8},{10,9... | collective-permute-start | bytes 2359304 | tf_op jit(solution)/shard_map/ppermute | solution.py:54
  54.8 9.6 %collective-permute-start.13 = (bf16[16,144,128]{2,1,0:T(8,128)(2,1)S(1)}, bf16[16,144,128]{2,1,0:T(8,128)(2,1)S(1)}, u32[]{:S(2)}, u32[]{:S(2)}) collective-permute-start(bf16[16,144,128]{2,1,0:T(8,128)(2,1)S(1)} %get-tuple-element.67), channel_id=1, source_target_pairs={{0,4},{4,0},{8,12},{12,8},{16,20},{20,16},{24,28},{28,24},{32,36},... | collective-permute-start | bytes 1769480 | tf_op jit(solution)/shard_map/ppermute | solution.py:78
